TPU v7x, 256 devices: a whole 4x4x8 slice. The times are simulated.
256 devices in a mesh: genome: 32 (over z, x), anc: 4 (over y_lo, core), trait: 2 (over y_hi).
Axes of the slice: x: 4, y: 4 (y_hi: 2, y_lo: 2; y = y_hi * 2 + y_lo), z: 8, core: 2. Of those that a mesh axis runs over, the one named last changes fastest.
Arguments:
- coefficients: float32 [4, 128, 65536], P('anc', 'trait', 'genome'), may hold values from -3 to 3
- sumstats: float32 [4, 128, 65536], P('anc', 'trait', 'genome'), may hold values from -12 to 12
- linkage: bfloat16 [4, 65536, 4096], P('anc', 'genome'), may hold values from -0.09375 to 0.09375
- band_start: int32 [4, 256], P('anc', 'genome'), may hold values from 0 to 61440, as said below
- group_ids: int32 [4, 65536], P('anc', 'genome'), may hold values from 0 to 63, never falling along the last dimension, each value on 1 to 8192 neighbouring positions
- group_weight: float32 [4, 64], P('anc'), may hold values from 0.1 to 1.5
- dosage: bfloat16 [4, 2048, 65536], P('anc', None, 'genome'), may hold values from 0 to 2
Outputs:
- updated: float32 [4, 128, 65536], P('anc', 'trait', 'genome')
- scores: float32 [4, 128, 2048], P('anc', 'trait', 'genome')
Inputs may be any that keep to these rules, and one draw needn't show every extreme that they name: band_start[a, u] is the first of the 4096 consecutive SNP columns stored in linkage[a] for row block u, the SNPs u * 256 to u * 256 + 255; these columns always include the block's own SNPs. `group_ids`: group ids never fall along the SNPs of an ancestry, so each group is one run of consecutive SNPs.
All inputs are finite; a program needn't handle non-finite values.
Results may differ from a plain program's by a relative error of at most 0.003.
Values may be sent and summed in bfloat16 or wider, within the bound.
No kernel may reach another device: no remote copies, remote signals or barrier semaphores. Data moves between devices by JAX's collectives and lax.ppermute only.
A program may use at most 128 MiB of HBM per device.

v0:
```python
import math

import jax
import jax.numpy as jnp
from jax import lax
from jax.sharding import PartitionSpec as P

TRAITS = 128
TILE = 256


step_size = 0.5
merging = 0.5
epsilon = 1e-06


def total_of_pieces(value, axis):
    parts = lax.all_gather(value, axis)
    return parts.sum(axis=0)


def passed_along(block, axis, distance):
    devices = range(lax.axis_size(axis))
    route = [(i - distance, i) for i in devices if i - distance in devices]
    return lax.ppermute(block, axis, route)


def sent_to_all(value, axis):
    copies = jnp.broadcast_to(value, (lax.axis_size(axis), *value.shape))
    return lax.all_to_all(copies, axis, split_axis=0, concat_axis=0, tiled=True)


def over_copies(value, axis):
    return sent_to_all(value, axis).sum(axis=0)


def rows_first(arrays, axis, dims):
    turned = [jnp.moveaxis(a, dim, 0) for a, dim in zip(arrays, dims)]
    both = jnp.concatenate([t.reshape(len(t), -1) for t in turned], axis=1)
    result, at, done = (lax.all_gather(both, axis, axis=0, tiled=True), 0, [])
    for t, dim in zip(turned, dims):
        piece = result[:, at : at + t[0].size].reshape(-1, *t.shape[1:])
        done.append(jnp.moveaxis(piece, 0, dim))
        at += t[0].size
    return tuple(done)


def cut_along(value, dim, peers):
    dims = value.shape
    parts = value.reshape(*dims[:dim], peers, dims[dim] // peers, *dims[dim + 1 :])
    return jnp.moveaxis(parts, dim, 0)


def sent_and_summed(value, axis, dim):
    parts = cut_along(value, dim, lax.axis_size(axis))
    arrived = lax.all_to_all(parts, axis, split_axis=0, concat_axis=0, tiled=True)
    return arrived.sum(axis=0)


def per_device(coefficients, sumstats, linkage, band_start, group_ids, group_weight, dosage):
    current = coefficients[0]
    targets = sumstats[0]
    band = linkage[0]
    starts = band_start[0]
    group_list = group_ids[0]
    weights = group_weight[0]
    genotype = dosage[0]
    traits_here, snp_rows = current.shape
    band_width = band.shape[1]
    reach_count = band_width // snp_rows
    genome_count = lax.axis_size("genome")
    position = lax.axis_index("genome")
    anchor = position * snp_rows
    ancestries = lax.axis_size("anc") * coefficients.shape[0]
    mean_coef = total_of_pieces(current, "anc") / ancestries
    low_copy = current.astype(jnp.bfloat16)
    below_list = []
    above_list = []
    for distance in range(1, reach_count + 1):
        below_list.insert(0, passed_along(low_copy, "genome", distance))
        above_list.append(passed_along(low_copy, "genome", -distance))
    extended = jnp.concatenate(below_list + [low_copy] + above_list, axis=1)
    local_start = starts - anchor + band_width
    windows = jax.vmap(
        lambda begin_at: lax.dynamic_slice_in_dim(extended, begin_at, band_width, 1)
    )(local_start)
    band_tiles = band.reshape(snp_rows // TILE, TILE, band_width)
    products = jnp.einsum("ntw,nrw->tnr", windows, band_tiles, preferred_element_type=jnp.float32)
    band_product = products.reshape(traits_here, snp_rows)
    gradient = current + band_product - targets + merging * (current - mean_coef)
    proposal = current - step_size * gradient
    trait_part = jnp.sum(proposal * proposal, axis=0)
    trait_total = over_copies(trait_part, "trait")
    same_group = (group_list[:, None] == group_list[None, :]).astype(jnp.float32)
    local_squares = jnp.dot(same_group, trait_total, precision=lax.Precision.HIGHEST)
    local_counts = jnp.sum(same_group, axis=1)
    id_float = group_list.astype(jnp.float32)
    first_id = id_float[0]
    last_id = id_float[-1]
    edge_values = rows_first(
        (
            first_id[None],
            last_id[None],
            local_squares[:1],
            local_counts[:1],
            local_squares[-1:],
            local_counts[-1:],
        ),
        "genome",
        (0, 0, 0, 0, 0, 0),
    )
    firsts, lasts, head_squares, head_counts, tail_squares, tail_counts = edge_values
    others = (jnp.arange(genome_count, dtype=jnp.int32) != position)[None, :]
    at_head = id_float[:, None] == firsts[None, :]
    at_tail = id_float[:, None] == lasts[None, :]
    square_terms = jnp.where(
        at_head, head_squares[None, :], jnp.where(at_tail, tail_squares[None, :], 0.0)
    )
    count_terms = jnp.where(
        at_head, head_counts[None, :], jnp.where(at_tail, tail_counts[None, :], 0.0)
    )
    extra_squares = jnp.sum(jnp.where(others, square_terms, 0.0), axis=1)
    extra_counts = jnp.sum(jnp.where(others, count_terms, 0.0), axis=1)
    group_squares = local_squares + extra_squares
    group_counts = local_counts + extra_counts
    lookup = (group_list[:, None] == jnp.arange(weights.shape[0], dtype=jnp.int32)[None, :]).astype(
        jnp.float32
    )
    snp_weight = jnp.dot(lookup, weights, precision=lax.Precision.HIGHEST)
    threshold = step_size * snp_weight * jnp.sqrt(group_counts * TRAITS)
    factor = jnp.maximum(0.0, 1.0 - threshold / jnp.sqrt(group_squares + epsilon))
    updated = proposal * factor[None, :]
    snps_total = snp_rows * genome_count
    partial_value = lax.dot_general(
        updated.astype(jnp.bfloat16),
        genotype,
        (((1,), (1,)), ((), ())),
        preferred_element_type=jnp.float32,
    ) / math.sqrt(snps_total)
    scores = sent_and_summed(partial_value, "genome", 1)
    return (updated[None], scores[None])


def solution(mesh):
    in_specs = (
        P("anc", "trait", "genome"),
        P("anc", "trait", "genome"),
        P("anc", "genome", None),
        P("anc", "genome"),
        P("anc", "genome"),
        P("anc", None),
        P("anc", None, "genome"),
    )
    out_specs = (P("anc", "trait", "genome"), P("anc", "trait", "genome"))
    return jax.shard_map(
        per_device, mesh=mesh, in_specs=in_specs, out_specs=out_specs, check_vma=False
    )
```

profile of v0, /device:TPU:8, one launch (start us, length us, event | category | flops | bytes accessed | tf_op | source)
XLA Modules:
  0.0 168.4 jit_solution(14491899200398587660)
XLA Ops:
  8.3 4.9 %collective-permute-start = (bf16[64,2048]{1,0:T(8,128)(2,1)S(1)}, bf16[64,2048]{1,0:T(8,128)(2,1)S(1)}, u32[]{:S(2)}, u32[]{:S(2)}) collective-permute-start(bf16[64,2048]{1,0:T(8,128)(2,1)S(1)} %bitcast_convert_fusion), channel_id=1, source_target_pairs={{0,16},{8,24},{16,32},{24,40},{32,48},{40,56},{48,64},{56,72},{64,... | collective-permute-start | bytes 786440 | tf_op jit(solution)/shard_map/ppermute | solution.py:25
  13.3 2.5 %collective-permute-start.1 = (bf16[64,2048]{1,0:T(8,128)(2,1)S(1)}, bf16[64,2048]{1,0:T(8,128)(2,1)S(1)}, u32[]{:S(2)}, u32[]{:S(2)}) collective-permute-start(bf16[64,2048]{1,0:T(8,128)(2,1)S(1)} %bitcast_convert_fusion), channel_id=1, source_target_pairs={{0,8},{8,16},{16,24},{24,32},{32,40},{40,48},{48,56},{56,64},{64,7... | collective-permute-start | bytes 786440 | tf_op jit(solution)/shard_map/ppermute | solution.py:25
  18.4 2.5 %fusion.2 = f32[2048]{0:T(1024)S(1)} fusion(s32[2048]{0:T(1024)} %bitcast.93), kind=kLoop, calls=%fused_computation.5 | loop fusion | flops 12580864 | bytes 16384 | tf_op jit(solution)/shard_map/reduce_sum | solution.py:96
  21.0 1.4 fusion.10
  26.7 3.7 %collective-permute-done.3 = bf16[64,2048]{1,0:T(8,128)(2,1)S(1)} collective-permute-done((bf16[64,2048]{1,0:T(8,128)(2,1)S(1)}, bf16[64,2048]{1,0:T(8,128)(2,1)S(1)}, u32[]{:S(2)}, u32[]{:S(2)}) %collective-permute-start.3) | collective-permute-done | bytes 262176 | tf_op jit(solution)/shard_map/ppermute | solution.py:25
  30.5 18.1 %while.1 = (s32[]{:T(128)}, bf16[64,10240]{1,0:T(8,128)(2,1)S(1)}, s32[8,2]{0,1:T(2,128)S(1)}, bf16[8,64,4096]{2,1,0:T(8,128)(2,1)}, s32[]{:T(128)}) while((s32[]{:T(128)}, bf16[64,10240]{1,0:T(8,128)(2,1)S(1)}, s32[8,2]{0,1:T(2,128)S(1)}, bf16[8,64,4096]{2,1,0:T(8,128)(2,1)}, s32[]{:T(128)}) %tuple.29), condition=%wide.while_cond, body=%wide.while_body.sunk | while | flops 2 | bytes 1049689 | solution.py:85
  31.1 1.6 bitcast_dynamic-update-slice_fusion.2
  33.4 1.7 bitcast_dynamic-update-slice_fusion.2
  35.6 1.7 bitcast_dynamic-update-slice_fusion.2
  37.9 1.7 bitcast_dynamic-update-slice_fusion.2
  40.2 1.6 bitcast_dynamic-update-slice_fusion.2
  42.4 1.7 bitcast_dynamic-update-slice_fusion.2
  44.7 1.6 bitcast_dynamic-update-slice_fusion.2
  47.0 1.7 bitcast_dynamic-update-slice_fusion.2
  48.6 12.4 %fusion.33 = f32[8,64,256]{2,1,0:T(8,128)S(1)} fusion(bf16[8,64,4096]{2,1,0:T(8,128)(2,1)} %get-tuple-element.9, bf16[8,256,4096]{2,1,0:T(8,128)(2,1)} %bitcast.83), kind=kOutput, calls=%fused_computation.59 | convolution fusion | flops 1073741824 | bytes 21495808 | tf_op jit(solution)/shard_map/ntw,nrw->tnr/dot_general | solution.py:88
  61.1 1.8 %reduce_sum.63 = f32[64,2048]{1,0:T(8,128)S(1)} reduce(f32[4,64,2048]{2,1,0:T(8,128)} %all-gather.3.cloned.1.call-done, f32[]{:T(128)} %constant.8.clone.1), dimensions={0}, to_apply=%region_0.0 | reduce | flops 393216 | bytes 2621444 | tf_op jit(solution)/shard_map/reduce_sum | solution.py:19
  63.8 3.6 %all-to-all-start = ((f32[2,1,2048]{2,1,0:T(1,128)}), f32[2,1,2048]{2,1,0:T(1,128)S(1)}, u32[]{:S(2)}, u32[]{:S(2)}) async-start(f32[2,1,2048]{2,1,0:T(1,128)} %broadcast_in_dim.67), calls=%async_computation | async-start | bytes 32768 | tf_op jit(solution)/shard_map/all_to_all | solution.py:30
  67.8 5.0 %all-to-all-done = f32[2,1,2048]{2,1,0:T(1,128)S(1)} async-done(((f32[2,1,2048]{2,1,0:T(1,128)}), f32[2,1,2048]{2,1,0:T(1,128)S(1)}, u32[]{:S(2)}, u32[]{:S(2)}) %all-to-all-start) | async-done | bytes 16416 | tf_op jit(solution)/shard_map/all_to_all | solution.py:30
  72.8 6.9 %fusion = f32[1,2048]{1,0:T(1,128)S(1)} fusion(f32[2048,1]{0,1:T(1,128)S(1)} %bitcast.92, s32[2048]{0:T(1024)S(1)} %bitcast.96), kind=kOutput, calls=%fused_computation.2 | convolution fusion | flops 54525952 | bytes 24576 | tf_op jit(solution)/shard_map/dot_general | solution.py:95
  80.3 3.9 %concatenate.11 = f32[1,6]{1,0:T(1,128)S(1)} concatenate(f32[1,1]{1,0:T(1,128)} %bitcast.10, f32[1,1]{1,0:T(1,128)} %bitcast.11, f32[1,1]{1,0:T(1,128)} %bitcast.15, f32[1,1]{1,0:T(1,128)} %bitcast.16, f32[1,1]{1,0:T(1,128)} %bitcast.17, f32[1,1]{1,0:T(1,128)} %bitcast.18), dimensions={1} | concatenate | bytes 48 | tf_op jit(solution)/shard_map/concatenate | solution.py:39
  84.2 45.6 %all-gather = f32[32,1,6]{2,1,0:T(1,128)S(1)} all-gather(f32[1,1,6]{2,1,0:T(1,128)S(1)} %bitcast.98), channel_id=1, replica_groups=mesh['genome'=32,'anc'=4,'trait'=2] {'genome'}, dimensions={0}, use_global_device_ids=true | all-gather | bytes 792 | tf_op jit(solution)/shard_map/all_gather | solution.py:40
  130.6 6.2 %fusion.7 = f32[64,2048]{1,0:T(8,128)S(1)} fusion(bf16[1,2048,2048]{2,1,0:T(8,128)(2,1)} %param.13, f32[1,64,2048]{2,1,0:T(8,128)S(1)} %fusion.20), kind=kOutput, calls=%fused_computation.10 | convolution fusion | flops 537133056 | bytes 9437184 | tf_op jit(solution)/shard_map/dot_general | solution.py:134
  138.5 19.5 %all_to_all.11 = f32[32,1,4096]{2,1,0:T(1,128)S(1)} all-to-all(f32[32,1,4096]{2,1,0:T(1,128)S(1)} %reshape.135), channel_id=1, replica_groups=mesh['genome'=32,'anc'=4,'trait'=2] {'genome'}, dimensions={0} | all-to-all | bytes 1048576 | tf_op jit(solution)/shard_map/all_to_all | solution.py:56
  158.5 1.9 %reduce.13 = f32[32,4096]{1,0:T(8,128)S(1)} reduce(f32[32,1,4096]{2,1,0:T(1,128)S(1)} %all_to_all.11, f32[]{:T(128)} %broadcast.110), dimensions={1}, to_apply=%all_to_all.8.reduce_sub_computation | reduce | bytes 1048580 | tf_op jit(solution)/shard_map/all_to_all | solution.py:56
  (64 shorter events, 18.8 us)
Async XLA Ops:
  7.2 13.8 %copy-start = (f32[1,64]{1,0:T(1,128)S(1)}, f32[1,64]{1,0:T(1,128)}, u32[]{:S(2)}) copy-start(f32[1,64]{1,0:T(1,128)} %param.12) | copy-start | bytes 772
  7.2 54.0 %all-gather.3.cloned.1.call-start = ((), (), s32[]{:S(2)}) async-start(), calls=%async_computation.2 | async-start | bytes 2621440 | tf_op jit(solution)/shard_map/all_gather | solution.py:18
  8.3 16.6 %collective-permute-start = (bf16[64,2048]{1,0:T(8,128)(2,1)S(1)}, bf16[64,2048]{1,0:T(8,128)(2,1)S(1)}, u32[]{:S(2)}, u32[]{:S(2)}) collective-permute-start(bf16[64,2048]{1,0:T(8,128)(2,1)S(1)} %bitcast_convert_fusion), channel_id=1, source_target_pairs={{0,16},{8,24},{16,32},{24,40},{32,48},{40,56},{48,64},{56,72},{64,... | collective-permute-start | bytes 786440 | tf_op jit(solution)/shard_map/ppermute | solution.py:25
  13.3 11.7 %collective-permute-start.1 = (bf16[64,2048]{1,0:T(8,128)(2,1)S(1)}, bf16[64,2048]{1,0:T(8,128)(2,1)S(1)}, u32[]{:S(2)}, u32[]{:S(2)}) collective-permute-start(bf16[64,2048]{1,0:T(8,128)(2,1)S(1)} %bitcast_convert_fusion), channel_id=1, source_target_pairs={{0,8},{8,16},{16,24},{24,32},{32,40},{40,48},{48,56},{56,64},{64,7... | collective-permute-start | bytes 786440 | tf_op jit(solution)/shard_map/ppermute | solution.py:25
  15.8 10.9 %collective-permute-start.2 = (bf16[64,2048]{1,0:T(8,128)(2,1)S(1)}, bf16[64,2048]{1,0:T(8,128)(2,1)S(1)}, u32[]{:S(2)}, u32[]{:S(2)}) collective-permute-start(bf16[64,2048]{1,0:T(8,128)(2,1)S(1)} %bitcast_convert_fusion), channel_id=1, source_target_pairs={{8,0},{16,8},{24,16},{32,24},{40,32},{48,40},{56,48},{64,56},{72,6... | collective-permute-start | bytes 786440 | tf_op jit(solution)/shard_map/ppermute | solution.py:25
  17.1 13.4 %collective-permute-start.3 = (bf16[64,2048]{1,0:T(8,128)(2,1)S(1)}, bf16[64,2048]{1,0:T(8,128)(2,1)S(1)}, u32[]{:S(2)}, u32[]{:S(2)}) collective-permute-start(bf16[64,2048]{1,0:T(8,128)(2,1)S(1)} %bitcast_convert_fusion), channel_id=1, source_target_pairs={{16,0},{24,8},{32,16},{40,24},{48,32},{56,40},{64,48},{72,56},{80,... | collective-permute-start | bytes 786440 | tf_op jit(solution)/shard_map/ppermute | solution.py:25
  48.6 14.3 %copy-start.1 = (f32[1,64,2048]{2,1,0:T(8,128)S(1)}, f32[1,64,2048]{2,1,0:T(8,128)}, u32[]{:S(2)}) copy-start(f32[1,64,2048]{2,1,0:T(8,128)} %param.7) | copy-start | bytes 1572868
  48.6 14.3 %copy-start.3 = (f32[1,64,2048]{2,1,0:T(8,128)S(1)}, f32[1,64,2048]{2,1,0:T(8,128)}, u32[]{:S(2)}) copy-start(f32[1,64,2048]{2,1,0:T(8,128)} %param.8) | copy-start | bytes 1572868
  61.1 11.7 %copy-start.4 = (s32[1,2048]{1,0:T(1,128)S(1)}, s32[1,2048]{1,0:T(1,128)}, u32[]{:S(2)}) copy-start(s32[1,2048]{1,0:T(1,128)} %param.11) | copy-start | bytes 24580
  63.8 9.0 %all-to-all-start = ((f32[2,1,2048]{2,1,0:T(1,128)}), f32[2,1,2048]{2,1,0:T(1,128)S(1)}, u32[]{:S(2)}, u32[]{:S(2)}) async-start(f32[2,1,2048]{2,1,0:T(1,128)} %broadcast_in_dim.67), calls=%async_computation | async-start | bytes 32768 | tf_op jit(solution)/shard_map/all_to_all | solution.py:30
  130.6 6.2 %copy-start.2 = (f32[1,64,2048]{2,1,0:T(8,128)}, f32[1,64,2048]{2,1,0:T(8,128)S(1)}, u32[]{:S(2)}) copy-start(f32[1,64,2048]{2,1,0:T(8,128)S(1)} %fusion.20) | copy-start | bytes 1572868
Sparse Core Ops, SparseCore 0:
  18.5 39.3 all-gather.2
where the time goes:
time: 169 us; the launch traced here: 168 us
  blocking collectives  65.1 us (39%)
  local copies, waits for them, and re-layouts  27.9 us (17%)
  matrix products  27 us (16%)
  between operations  14.3 us (8%)
  starting transfers between devices  13.7 us (8%)
  other arithmetic  11.1 us (7%)
  waiting for transfers between devices  9.33 us (6%)
    all_gather x1, blocking collectives, rows_first(): result, at, done = (lax.all_gather(both, axis, axis=0, tiled=True), 0, [])  45.6 us
    all_to_all x1, blocking collectives, sent_and_summed(): lax.all_to_all(parts, axis, split_axis=0, concat_axis=0, tiled=True)  19.5 us
    gather x24, local copies, waits for them, and re-layouts  18.1 us
    dot_general x1, matrix products, per_device(): jnp.einsum('ntw,nrw->tnr', windows, band_tiles, preferred_element_type=jn...  12.4 us
    ppermute x4, starting transfers between devices, passed_along(): return lax.ppermute(block, axis, route)  10 us
    dot_general x1, matrix products, per_device(): jnp.dot(same_group, trait_total, precision=lax.Precision.HIGHEST)  6.93 us
    dot_general x1, matrix products, per_device(): lax.dot_general(updated.astype(jnp.bfloat16), genotype, (((1,), (1,)), ((...  6.23 us
    all_to_all x1, waiting for transfers between devices, sent_to_all(): return lax.all_to_all(copies, axis, split_axis=0, concat_axis=0, tiled=True)  4.96 us
  transfers between devices with their start and end apart: 6, of which 3 were waited for; matrix products, arithmetic and copies ran while one was open for 23% of the time, Pallas kernels for 0%

commit v1 on v0

v1 whole, which is shorter than its diff:
```python
import functools
import math

import jax
import jax.numpy as jnp
from jax import lax
from jax.experimental import pallas as pl
from jax.experimental.pallas import tpu as pltpu
from jax.sharding import PartitionSpec as P

TILE = 256
LANES = 128
GROUPS = 64

step_size = 0.5
merging = 0.5
epsilon = 1e-06

NT = (((1,), (1,)), ((), ()))


def band_kernel(
    ancestries, starts, far_below, below, own, above, far_above, band, coef, targets, anc1, anc2, anc3, ids,
    proposal, sums, extended, square_acc, count_acc,
):
    unit = pl.program_id(0)
    rows, snps = own.shape
    width = band.shape[1]

    @pl.when(unit == 0)
    def _():
        for at, piece in enumerate((far_below, below, own, above, far_above)):
            extended[:, at * snps : (at + 1) * snps] = piece[...].astype(jnp.float32)
        extended[:, 5 * snps :] = jnp.zeros((rows, LANES), jnp.float32)
        square_acc[...] = jnp.zeros_like(square_acc)
        count_acc[...] = jnp.zeros_like(count_acc)

    start = starts[unit]
    base = pl.multiple_of((start // LANES) * LANES, LANES)
    shift = start - base
    back = lax.rem(LANES - shift, LANES)
    lane = lax.broadcasted_iota(jnp.int32, (rows, LANES), 1)
    keep = lane < LANES - shift
    window = []
    turned = pltpu.roll(extended[:, pl.ds(base, LANES)], back, 1)
    for at in range(width // LANES):
        following = pltpu.roll(extended[:, pl.ds(base + (at + 1) * LANES, LANES)], back, 1)
        window.append(jnp.where(keep, turned, following).astype(jnp.bfloat16))
        turned = following
    window = jnp.concatenate(window, axis=1)
    product = lax.dot_general(window, band[...], NT, preferred_element_type=jnp.float32)

    current = coef[...]
    total = current + anc1[...].astype(jnp.float32) + anc2[...].astype(jnp.float32) + anc3[...].astype(jnp.float32)
    gradient = current + product - targets[...] + merging * (current - total * (1.0 / ancestries))
    value = current - step_size * gradient
    proposal[...] = value
    part = jnp.sum(value * value, axis=0, keepdims=True)
    group = lax.broadcasted_iota(jnp.int32, (GROUPS, LANES), 0)
    squares = square_acc[...]
    counts = count_acc[...]
    for at in range(TILE // LANES):
        here = ids[:, at * LANES : (at + 1) * LANES] == group
        squares += jnp.where(here, part[:, at * LANES : (at + 1) * LANES], 0.0)
        counts += jnp.where(here, 1.0, 0.0)
    square_acc[...] = squares
    count_acc[...] = counts

    @pl.when(unit == pl.num_programs(0) - 1)
    def _():
        place = lax.broadcasted_iota(jnp.int32, (GROUPS, LANES), 1)
        square_col = jnp.sum(squares, axis=1, keepdims=True)
        count_col = jnp.sum(counts, axis=1, keepdims=True)
        both = jnp.where(place == group, square_col, 0.0) + jnp.where(place == group + GROUPS, count_col * rows, 0.0)
        sums[...] = jnp.broadcast_to(jnp.sum(both, axis=0, keepdims=True), sums.shape)


def band_step(starts, pieces, band, coef, targets, ancs, ids, peers, ancestries):
    rows, snps = coef.shape
    width = band.shape[1]
    whole = pl.BlockSpec((rows, snps), lambda u: (0, 0))
    tile = pl.BlockSpec((rows, TILE), lambda u: (0, u))
    return pl.pallas_call(
        functools.partial(band_kernel, ancestries),
        grid=(snps // TILE,),
        in_specs=[pl.BlockSpec(memory_space=pltpu.SMEM)]
        + [whole] * 5
        + [pl.BlockSpec((TILE, width), lambda u: (u, 0)), tile, tile, tile, tile, tile,
           pl.BlockSpec((1, TILE), lambda u: (0, u))],
        out_specs=[tile, pl.BlockSpec((peers, LANES), lambda u: (0, 0))],
        out_shape=[
            jax.ShapeDtypeStruct((rows, snps), jnp.float32),
            jax.ShapeDtypeStruct((peers, LANES), jnp.float32),
        ],
        scratch_shapes=[
            pltpu.VMEM((rows, 5 * snps + LANES), jnp.float32),
            pltpu.VMEM((GROUPS, LANES), jnp.float32),
            pltpu.VMEM((GROUPS, LANES), jnp.float32),
        ],
        compiler_params=pltpu.CompilerParams(
            dimension_semantics=("arbitrary",), vmem_limit_bytes=52 << 20
        ),
        cost_estimate=pl.CostEstimate(
            flops=2 * rows * snps * width, bytes_accessed=2 * snps * width + 24 * rows * snps, transcendentals=0
        ),
        name="band_step",
    )(starts, *pieces, band, coef, targets, *ancs, ids)


def score_kernel(scale, sums, weights, ids, proposal, dosage, updated, partial, low):
    rows, snps = proposal.shape

    @pl.when(pl.program_id(0) == 0)
    def _():
        total = jnp.sum(sums[...], axis=0, keepdims=True)
        spread = jnp.broadcast_to(total, (GROUPS, LANES))
        group = lax.broadcasted_iota(jnp.int32, (GROUPS, LANES), 0)
        place = lax.broadcasted_iota(jnp.int32, (GROUPS, LANES), 1)
        squares = jnp.sum(jnp.where(place == group, spread, 0.0), axis=1, keepdims=True)
        counts = jnp.sum(jnp.where(place == group + GROUPS, spread, 0.0), axis=1, keepdims=True)
        weight_row = jnp.broadcast_to(weights[...], (GROUPS, GROUPS))
        here = lax.broadcasted_iota(jnp.int32, (GROUPS, GROUPS), 0) == lax.broadcasted_iota(
            jnp.int32, (GROUPS, GROUPS), 1
        )
        weight = jnp.sum(jnp.where(here, weight_row, 0.0), axis=1, keepdims=True)
        threshold = step_size * weight * jnp.sqrt(counts)
        factor = jnp.maximum(0.0, 1.0 - threshold / jnp.sqrt(squares + epsilon))
        factor = jnp.broadcast_to(factor, (GROUPS, LANES))
        for at in range(snps // LANES):
            cut = slice(at * LANES, (at + 1) * LANES)
            chosen = jnp.sum(jnp.where(ids[:, cut] == group, factor, 0.0), axis=0, keepdims=True)
            value = proposal[:, cut] * chosen
            updated[:, cut] = value
            low[:, cut] = value.astype(jnp.bfloat16)

    product = lax.dot_general(low[...], dosage[...], NT, preferred_element_type=jnp.float32) * scale
    half = rows // 2
    left = lax.broadcasted_iota(jnp.int32, (half, LANES), 1) < LANES // 2
    for at in range(product.shape[1] // LANES):
        cut = product[:, at * LANES : (at + 1) * LANES]
        first, second = cut[:half], cut[half:]
        partial[2 * at] = jnp.where(left, first, pltpu.roll(second, LANES // 2, 1)).astype(partial.dtype)
        partial[2 * at + 1] = jnp.where(left, pltpu.roll(first, LANES // 2, 1), second).astype(partial.dtype)


def score_step(sums, weights, ids, proposal, dosage, genome_count):
    rows, snps = proposal.shape
    persons = dosage.shape[0]
    block = 256
    each = persons // genome_count
    whole = pl.BlockSpec((rows, snps), lambda p: (0, 0))
    return pl.pallas_call(
        functools.partial(score_kernel, 1.0 / math.sqrt(snps * genome_count)),
        grid=(persons // block,),
        in_specs=[
            pl.BlockSpec(sums.shape, lambda p: (0, 0)),
            pl.BlockSpec((1, GROUPS), lambda p: (0, 0)),
            pl.BlockSpec((1, snps), lambda p: (0, 0)),
            whole,
            pl.BlockSpec((block, snps), lambda p: (p, 0)),
        ],
        out_specs=[whole, pl.BlockSpec((block // each, rows // 2, LANES), lambda p: (p, 0, 0))],
        out_shape=[
            jax.ShapeDtypeStruct((rows, snps), jnp.float32),
            jax.ShapeDtypeStruct((genome_count, rows // 2, LANES), jnp.bfloat16),
        ],
        scratch_shapes=[pltpu.VMEM((rows, snps), jnp.bfloat16)],
        compiler_params=pltpu.CompilerParams(
            dimension_semantics=("arbitrary",), vmem_limit_bytes=32 << 20
        ),
        cost_estimate=pl.CostEstimate(
            flops=2 * rows * snps * persons, bytes_accessed=2 * snps * persons + 8 * rows * snps, transcendentals=0
        ),
        name="score_step",
    )(sums, weights, ids, proposal, dosage)


def total_kernel(arrived, scores):
    total = jnp.sum(arrived[...].astype(jnp.float32), axis=0)
    half = LANES // 2
    rows = total.shape[0]
    scores[:rows] = total[:, :half]
    scores[rows:] = pltpu.roll(total, half, 1)[:, :half]


def total_step(arrived):
    rows = 2 * arrived.shape[1]
    return pl.pallas_call(
        total_kernel,
        out_shape=jax.ShapeDtypeStruct((rows, LANES // 2), jnp.float32),
        name="total_step",
    )(arrived)


def passed_along(block, axis, distance):
    devices = range(lax.axis_size(axis))
    route = [(i - distance, i) for i in devices if i - distance in devices]
    return lax.ppermute(block, axis, route)


def per_device(coefficients, sumstats, linkage, band_start, group_ids, group_weight, dosage):
    current = coefficients[0]
    targets = sumstats[0]
    band = linkage[0]
    starts = band_start[0]
    snp_rows = current.shape[1]
    genome_count = lax.axis_size("genome")
    anc_count = lax.axis_size("anc")
    position = lax.axis_index("genome")
    low_copy = current.astype(jnp.bfloat16)
    pieces = [
        passed_along(low_copy, "genome", 2),
        passed_along(low_copy, "genome", 1),
        low_copy,
        passed_along(low_copy, "genome", -1),
        passed_along(low_copy, "genome", -2),
    ]
    ancs = [
        lax.ppermute(low_copy, "anc", [(i, i ^ k) for i in range(anc_count)]) for k in range(1, anc_count)
    ]
    local_start = starts - position * snp_rows + 2 * snp_rows
    peers = genome_count * lax.axis_size("trait")
    proposal, sums = band_step(
        local_start, pieces, band, current, targets, ancs, group_ids, peers, anc_count
    )
    arrived = lax.all_to_all(
        sums.reshape(peers, 1, LANES), ("genome", "trait"), split_axis=0, concat_axis=0, tiled=True
    ).reshape(peers, LANES)
    updated, partial = score_step(arrived, group_weight, group_ids, proposal, dosage[0], genome_count)
    received = lax.all_to_all(partial, "genome", split_axis=0, concat_axis=0, tiled=True)
    scores = total_step(received)
    return (updated[None], scores[None])


def solution(mesh):
    in_specs = (
        P("anc", "trait", "genome"),
        P("anc", "trait", "genome"),
        P("anc", "genome", None),
        P("anc", "genome"),
        P("anc", "genome"),
        P("anc", None),
        P("anc", None, "genome"),
    )
    out_specs = (P("anc", "trait", "genome"), P("anc", "trait", "genome"))
    return jax.shard_map(
        per_device, mesh=mesh, in_specs=in_specs, out_specs=out_specs, check_vma=False
    )
```

time: 169 us -> 90.4 us (0.53)
  matrix products: 27 us -> 0 us
  local copies, waits for them, and re-layouts: 27.9 us -> 1.75 us
  blocking collectives: 65.1 us -> 42.4 us
  Pallas kernels: 0 us -> 18.9 us
  between operations: 14.3 us -> 0.73 us
  other arithmetic: 11.1 us -> 1.89 us
    all_gather x1 -> x0, blocking collectives: 45.6 us -> none  [rows_first(): result, at, done = (lax.all_gather(both, axis, axis=0, tiled=True), 0, [])]
    dot_general x4 -> x0, matrix products: 27 us -> none  [the longest x1 12.4 us: per_device(): jnp.einsum('ntw,nrw->tnr', windows, band_tiles, preferred_element_type=jn...]
    all_to_all x1 -> x2, blocking collectives: 19.5 us -> 42.4 us  [the longest x1 27 us: per_device(): lax.all_to_all(sums.reshape(peers, 1, LANES), ('genome', 'trait'), split_...]
    pallas_call x0 -> x3, Pallas kernels: none -> 18.9 us  [the longest x1 12.4 us: band_step(): pl.pallas_call(functools.partial(band_kernel, ancestries), grid=(snps //...]
    gather x24 -> x0, local copies, waits for them, and re-layouts: 18.1 us -> none
    reduce_sum x6 -> x0, other arithmetic: 5.47 us -> none  [the longest x1 2.54 us: per_device(): local_counts = jnp.sum(same_group, axis=1)]
    ppermute x0 -> x3, waiting for transfers between devices: none -> 5.24 us  [per_device(): lax.ppermute(low_copy, 'anc', [(i, i ^ k) for i in range(anc_count)])]
    all_to_all x1 -> x0, waiting for transfers between devices: 4.96 us -> none  [sent_to_all(): return lax.all_to_all(copies, axis, split_axis=0, concat_axis=0, tiled=True)]
  transfers between devices with their start and end apart: 6 -> 7, of which waited for: 3 -> 3; matrix products, arithmetic and copies ran while one was open for 23% -> 1% of each run, Pallas kernels for 0% -> 0%
where the time goes in v1:
time: 90.4 us; the launch traced here: 89.9 us
  blocking collectives  42.4 us (47%)
  Pallas kernels  18.9 us (21%)
  starting transfers between devices  14 us (15%)
  waiting for transfers between devices  10.2 us (11%)
  other arithmetic  1.89 us (2%)
  local copies, waits for them, and re-layouts  1.75 us (2%)
    all_to_all x1, blocking collectives, per_device(): lax.all_to_all(sums.reshape(peers, 1, LANES), ('genome', 'trait'), split_...  27 us
    all_to_all x1, blocking collectives, per_device(): lax.all_to_all(partial, 'genome', split_axis=0, concat_axis=0, tiled=True)  15.5 us
    pallas_call x1, Pallas kernels, band_step(): pl.pallas_call(functools.partial(band_kernel, ancestries), grid=(snps //...  12.4 us
    ppermute x4, starting transfers between devices, passed_along(): return lax.ppermute(block, axis, route)  11.6 us
    ppermute x3, waiting for transfers between devices, per_device(): lax.ppermute(low_copy, 'anc', [(i, i ^ k) for i in range(anc_count)])  5.24 us
    ppermute x4, waiting for transfers between devices, passed_along(): return lax.ppermute(block, axis, route)  4.95 us
    pallas_call x1, Pallas kernels, score_step(): pl.pallas_call(functools.partial(score_kernel, 1.0 / math.sqrt(snps * gen...  4.82 us
    ppermute x3, starting transfers between devices, per_device(): lax.ppermute(low_copy, 'anc', [(i, i ^ k) for i in range(anc_count)])  2.38 us
  transfers between devices with their start and end apart: 7, of which 3 were waited for; matrix products, arithmetic and copies ran while one was open for 1% of the time, Pallas kernels for 0%

profile of v1, /device:TPU:8, one launch (start us, length us, event | category | flops | bytes accessed | tf_op | source)
XLA Modules:
  0.0 89.9 jit_solution(9834398817472355797)
XLA Ops:
  0.6 1.1 %bitcast_convert_fusion.own = bf16[64,2048]{1,0:T(8,128)(2,1)S(1)} fusion(f32[1,64,2048]{2,1,0:T(8,128)} %param.7), kind=kLoop, calls=%fused_computation.1 | loop fusion | flops 131072 | bytes 786432 | tf_op jit(solution)/shard_map/convert_element_type | solution.py:210
  1.7 0.1 collective-permute-start.6
  1.8 2.3 %collective-permute-start.5 = (bf16[64,2048]{1,0:T(8,128)(2,1)S(1)}, bf16[64,2048]{1,0:T(8,128)(2,1)S(1)}, u32[]{:S(2)}, u32[]{:S(2)}) collective-permute-start(bf16[64,2048]{1,0:T(8,128)(2,1)S(1)} %bitcast_convert_fusion.own), channel_id=1, source_target_pairs={{0,4},{2,6},{4,0},{6,2},{1,5},{3,7},{5,1},{7,3},{8,12},{10,14},{12... | collective-permute-start | bytes 786440 | tf_op jit(solution)/shard_map/ppermute | solution.py:219
  4.1 0.0 collective-permute-start.4
  4.1 1.3 %collective-permute-start.3 = (bf16[64,2048]{1,0:T(8,128)(2,1)S(1)}, bf16[64,2048]{1,0:T(8,128)(2,1)S(1)}, u32[]{:S(2)}, u32[]{:S(2)}) collective-permute-start(bf16[64,2048]{1,0:T(8,128)(2,1)S(1)} %bitcast_convert_fusion.own), channel_id=1, source_target_pairs={{16,0},{24,8},{32,16},{40,24},{48,32},{56,40},{64,48},{72,56},{80,... | collective-permute-start | bytes 786440 | tf_op jit(solution)/shard_map/ppermute | solution.py:198
  5.4 1.3 %collective-permute-start.2 = (bf16[64,2048]{1,0:T(8,128)(2,1)S(1)}, bf16[64,2048]{1,0:T(8,128)(2,1)S(1)}, u32[]{:S(2)}, u32[]{:S(2)}) collective-permute-start(bf16[64,2048]{1,0:T(8,128)(2,1)S(1)} %bitcast_convert_fusion.own), channel_id=1, source_target_pairs={{8,0},{16,8},{24,16},{32,24},{40,32},{48,40},{56,48},{64,56},{72,6... | collective-permute-start | bytes 786440 | tf_op jit(solution)/shard_map/ppermute | solution.py:198
  6.7 3.0 %collective-permute-done.6.anc3 = bf16[64,2048]{1,0:T(8,128)(2,1)S(1)} collective-permute-done((bf16[64,2048]{1,0:T(8,128)(2,1)S(1)}, bf16[64,2048]{1,0:T(8,128)(2,1)S(1)}, u32[]{:S(2)}, u32[]{:S(2)}) %collective-permute-start.6) | collective-permute-done | bytes 262176 | tf_op jit(solution)/shard_map/ppermute | solution.py:219
  9.7 4.1 %collective-permute-start.1 = (bf16[64,2048]{1,0:T(8,128)(2,1)S(1)}, bf16[64,2048]{1,0:T(8,128)(2,1)S(1)}, u32[]{:S(2)}, u32[]{:S(2)}) collective-permute-start(bf16[64,2048]{1,0:T(8,128)(2,1)S(1)} %bitcast_convert_fusion.own), channel_id=1, source_target_pairs={{0,8},{8,16},{16,24},{24,32},{32,40},{40,48},{48,56},{56,64},{64,7... | collective-permute-start | bytes 786440 | tf_op jit(solution)/shard_map/ppermute | solution.py:198
  13.8 2.2 %collective-permute-done.5.anc2 = bf16[64,2048]{1,0:T(8,128)(2,1)S(1)} collective-permute-done((bf16[64,2048]{1,0:T(8,128)(2,1)S(1)}, bf16[64,2048]{1,0:T(8,128)(2,1)S(1)}, u32[]{:S(2)}, u32[]{:S(2)}) %collective-permute-start.5) | collective-permute-done | bytes 262176 | tf_op jit(solution)/shard_map/ppermute | solution.py:219
  16.0 4.9 %collective-permute-start = (bf16[64,2048]{1,0:T(8,128)(2,1)S(1)}, bf16[64,2048]{1,0:T(8,128)(2,1)S(1)}, u32[]{:S(2)}, u32[]{:S(2)}) collective-permute-start(bf16[64,2048]{1,0:T(8,128)(2,1)S(1)} %bitcast_convert_fusion.own), channel_id=1, source_target_pairs={{0,16},{8,24},{16,32},{24,40},{32,48},{40,56},{48,64},{56,72},{64,... | collective-permute-start | bytes 786440 | tf_op jit(solution)/shard_map/ppermute | solution.py:198
  21.0 0.0 slice-start
  21.0 0.8 add_bitcast_fusion.starts
  21.8 0.0 collective-permute-done.4.anc1
  21.8 0.0 collective-permute-done.3.far_above
  21.8 0.0 collective-permute-done.2.above
  21.8 4.9 %collective-permute-done.far_below = bf16[64,2048]{1,0:T(8,128)(2,1)S(1)} collective-permute-done((bf16[64,2048]{1,0:T(8,128)(2,1)S(1)}, bf16[64,2048]{1,0:T(8,128)(2,1)S(1)}, u32[]{:S(2)}, u32[]{:S(2)}) %collective-permute-start) | collective-permute-done | bytes 262176 | tf_op jit(solution)/shard_map/ppermute | solution.py:198
  26.8 0.7 copy-done.1
  27.5 12.4 %band_step.1 = (f32[64,2048]{1,0:T(8,128)}, f32[64,128]{1,0:T(8,128)S(1)}) custom-call(s32[8]{0:T(128)S(1)} %add_bitcast_fusion.starts, bf16[64,2048]{1,0:T(8,128)(2,1)S(1)} %collective-permute-done.far_below, bf16[64,2048]{1,0:T(8,128)(2,1)S(1)} %collective-permute-done.1.below, bf16[64,2048]{1,0:T(8,128)(2,1)S(1)} %bitcast_convert_fusion.own, ...), custom_call_target="tpu_custom_call" | custom-call | flops 1073741824 | bytes 19922944 | tf_op jit(solution)/shard_map/band_step/pallas_call | solution.py:83
  39.9 27.0 %all_to_all.10 = f32[64,1,128]{2,1,0:T(1,128)S(1)} all-to-all(f32[64,1,128]{2,1,0:T(1,128)S(1)} %bitcast.17), channel_id=1, replica_groups=mesh['genome'=32,'anc'=4,'trait'=2] {'genome','trait'}, dimensions={0} | all-to-all | bytes 65536 | tf_op jit(solution)/shard_map/all_to_all | solution.py:226
  66.9 0.0 copy-start
  66.9 1.0 %copy-done = f32[64,2048]{1,0:T(8,128)S(1)} copy-done((f32[64,2048]{1,0:T(8,128)S(1)}, f32[64,2048]{1,0:T(8,128)}, u32[]{:S(2)}) %copy-start) | copy-done | bytes 524312
  67.9 4.8 %score_step.1 = (f32[64,2048]{1,0:T(8,128)}, bf16[32,32,128]{2,1,0:T(8,128)(2,1)S(1)}) custom-call(f32[64,128]{1,0:T(8,128)S(1)} %bitcast.16, f32[1,64]{1,0:T(1,128)S(1)} %copy-done.2, s32[1,2048]{1,0:T(1,128)S(1)} %copy-done.1, f32[64,2048]{1,0:T(8,128)S(1)} %copy-done, bf16[2048,2048]{1,0:T(8,128)(2,1)S(1)} %bitcast.15), custom_call_target="tpu_custom_call" | custom-call | flops 536870912 | bytes 9437184 | tf_op jit(solution)/shard_map/score_step/pallas_call | solution.py:152
  72.7 15.5 %all_to_all.11.arrived = bf16[32,32,128]{2,1,0:T(8,128)(2,1)} all-to-all(bf16[32,32,128]{2,1,0:T(8,128)(2,1)S(1)} %get-tuple-element.9), channel_id=1, replica_groups=mesh['genome'=32,'anc'=4,'trait'=2] {'genome'}, dimensions={0} | all-to-all | bytes 524288 | tf_op jit(solution)/shard_map/all_to_all | solution.py:230
  88.2 1.7 %total_step.1 = f32[64,64]{1,0:T(8,128)} custom-call(bf16[32,32,128]{2,1,0:T(8,128)(2,1)} %all_to_all.11.arrived), custom_call_target="tpu_custom_call" | custom-call | tf_op jit(solution)/shard_map/total_step/pallas_call | solution.py:188
  (10 shorter events, 0.0 us)
Async XLA Ops:
  0.6 66.2 %copy-start.2 = (f32[1,64]{1,0:T(1,128)S(1)}, f32[1,64]{1,0:T(1,128)}, u32[]{:S(2)}) copy-start(f32[1,64]{1,0:T(1,128)} %weights.1) | copy-start | bytes 772
  1.7 8.0 %collective-permute-start.6 = (bf16[64,2048]{1,0:T(8,128)(2,1)S(1)}, bf16[64,2048]{1,0:T(8,128)(2,1)S(1)}, u32[]{:S(2)}, u32[]{:S(2)}) collective-permute-start(bf16[64,2048]{1,0:T(8,128)(2,1)S(1)} %bitcast_convert_fusion.own), channel_id=1, source_target_pairs={{0,6},{2,4},{4,2},{6,0},{1,7},{3,5},{5,3},{7,1},{8,14},{10,12},{12... | collective-permute-start | bytes 786440 | tf_op jit(solution)/shard_map/ppermute | solution.py:219
  1.8 14.2 %collective-permute-start.5 = (bf16[64,2048]{1,0:T(8,128)(2,1)S(1)}, bf16[64,2048]{1,0:T(8,128)(2,1)S(1)}, u32[]{:S(2)}, u32[]{:S(2)}) collective-permute-start(bf16[64,2048]{1,0:T(8,128)(2,1)S(1)} %bitcast_convert_fusion.own), channel_id=1, source_target_pairs={{0,4},{2,6},{4,0},{6,2},{1,5},{3,7},{5,1},{7,3},{8,12},{10,14},{12... | collective-permute-start | bytes 786440 | tf_op jit(solution)/shard_map/ppermute | solution.py:219
  4.1 17.7 %collective-permute-start.4 = (bf16[64,2048]{1,0:T(8,128)(2,1)S(1)}, bf16[64,2048]{1,0:T(8,128)(2,1)S(1)}, u32[]{:S(2)}, u32[]{:S(2)}) collective-permute-start(bf16[64,2048]{1,0:T(8,128)(2,1)S(1)} %bitcast_convert_fusion.own), channel_id=1, source_target_pairs={{0,2},{2,0},{4,6},{6,4},{1,3},{3,1},{5,7},{7,5},{8,10},{10,8},{12,... | collective-permute-start | bytes 786440 | tf_op jit(solution)/shard_map/ppermute | solution.py:219
  4.1 17.7 %collective-permute-start.3 = (bf16[64,2048]{1,0:T(8,128)(2,1)S(1)}, bf16[64,2048]{1,0:T(8,128)(2,1)S(1)}, u32[]{:S(2)}, u32[]{:S(2)}) collective-permute-start(bf16[64,2048]{1,0:T(8,128)(2,1)S(1)} %bitcast_convert_fusion.own), channel_id=1, source_target_pairs={{16,0},{24,8},{32,16},{40,24},{48,32},{56,40},{64,48},{72,56},{80,... | collective-permute-start | bytes 786440 | tf_op jit(solution)/shard_map/ppermute | solution.py:198
  5.4 16.4 %collective-permute-start.2 = (bf16[64,2048]{1,0:T(8,128)(2,1)S(1)}, bf16[64,2048]{1,0:T(8,128)(2,1)S(1)}, u32[]{:S(2)}, u32[]{:S(2)}) collective-permute-start(bf16[64,2048]{1,0:T(8,128)(2,1)S(1)} %bitcast_convert_fusion.own), channel_id=1, source_target_pairs={{8,0},{16,8},{24,16},{32,24},{40,32},{48,40},{56,48},{64,56},{72,6... | collective-permute-start | bytes 786440 | tf_op jit(solution)/shard_map/ppermute | solution.py:198
  9.7 17.1 %copy-start.3 = (bf16[64,2048]{1,0:T(8,128)(2,1)}, bf16[64,2048]{1,0:T(8,128)(2,1)S(1)}, u32[]{:S(2)}) copy-start(bf16[64,2048]{1,0:T(8,128)(2,1)S(1)} %collective-permute-done.6.anc3) | copy-start | bytes 786436
  9.7 12.1 %collective-permute-start.1 = (bf16[64,2048]{1,0:T(8,128)(2,1)S(1)}, bf16[64,2048]{1,0:T(8,128)(2,1)S(1)}, u32[]{:S(2)}, u32[]{:S(2)}) collective-permute-start(bf16[64,2048]{1,0:T(8,128)(2,1)S(1)} %bitcast_convert_fusion.own), channel_id=1, source_target_pairs={{0,8},{8,16},{16,24},{24,32},{32,40},{40,48},{48,56},{56,64},{64,7... | collective-permute-start | bytes 786440 | tf_op jit(solution)/shard_map/ppermute | solution.py:198
  16.0 10.7 %collective-permute-start = (bf16[64,2048]{1,0:T(8,128)(2,1)S(1)}, bf16[64,2048]{1,0:T(8,128)(2,1)S(1)}, u32[]{:S(2)}, u32[]{:S(2)}) collective-permute-start(bf16[64,2048]{1,0:T(8,128)(2,1)S(1)} %bitcast_convert_fusion.own), channel_id=1, source_target_pairs={{0,16},{8,24},{16,32},{24,40},{32,48},{40,56},{48,64},{56,72},{64,... | collective-permute-start | bytes 786440 | tf_op jit(solution)/shard_map/ppermute | solution.py:198
  21.0 45.9 %slice-start = ((s8[8388608]{0:T(1024)(128)(4,1)}), s8[4194304]{0:T(1024)(128)(4,1)S(1)}, s32[]{:S(2)}) async-start(s8[8388608]{0:T(1024)(128)(4,1)} %bitcast.13), calls=%async_computation.2 | async-start | bytes 8388608
  26.8 0.7 copy-start.1
  27.5 39.4 %slice-start.1 = ((s8[8388608]{0:T(1024)(128)(4,1)}), s8[4194304]{0:T(1024)(128)(4,1)S(1)}, s32[]{:S(2)}) async-start(s8[8388608]{0:T(1024)(128)(4,1)} %bitcast.13), calls=%async_computation.3 | async-start | bytes 8388608
  66.9 1.0 %copy-start = (f32[64,2048]{1,0:T(8,128)S(1)}, f32[64,2048]{1,0:T(8,128)}, u32[]{:S(2)}) copy-start(f32[64,2048]{1,0:T(8,128)} %get-tuple-element.7.proposal) | copy-start | bytes 1572868

commit v2 on v1

--- a/solution.py
+++ b/solution.py
@@ -19,92 +19,192 @@
 NT = (((1,), (1,)), ((), ()))
 
 
-def band_kernel(
-    ancestries, starts, far_below, below, own, above, far_above, band, coef, targets, anc1, anc2, anc3, ids,
-    proposal, sums, extended, square_acc, count_acc,
-):
-    unit = pl.program_id(0)
+def place_of():
+    return lax.axis_index("genome")
+
+
+def cast_kernel(coef, low, first, second):
+    skip = jnp.where(lax.rem(place_of(), 4) < 2, TILE, 0)
+    low[...] = coef[...].astype(jnp.bfloat16)
+    for begin, out in ((skip, first), (TILE - skip, second)):
+        out[...] = coef[:, pl.ds(pl.multiple_of(begin, TILE), out.shape[1])].astype(jnp.bfloat16)
+
+
+def cast_step(coef):
+    rows, snps = coef.shape
+    part = jax.ShapeDtypeStruct((rows, snps - TILE), jnp.bfloat16)
+    vmem = pl.BlockSpec(memory_space=pltpu.VMEM)
+    return pl.pallas_call(
+        cast_kernel,
+        in_specs=[vmem],
+        out_specs=[vmem] * 3,
+        out_shape=[jax.ShapeDtypeStruct((rows, snps), jnp.bfloat16), part, part],
+        name="cast_step",
+    )(coef)
+
+
+def window_tiles(source, base, shift, count):
+    rows = source.shape[0]
+    back = lax.rem(LANES - shift, LANES)
+    keep = lax.broadcasted_iota(jnp.int32, (rows, LANES), 1) < LANES - shift
+    tiles = []
+    turned = pltpu.roll(source[:, pl.ds(base, LANES)], back, 1)
+    for at in range(count):
+        following = pltpu.roll(source[:, pl.ds(base + (at + 1) * LANES, LANES)], back, 1)
+        tiles.append(jnp.where(keep, turned, following).astype(jnp.bfloat16))
+        turned = following
+    return jnp.concatenate(tiles, axis=1)
+
+
+def near_kernel(starts, own, first, second, band, product, held, extended, sems):
+    rows, snps = own.shape
+    place = place_of()
+    above_first = lax.rem(place, 2) == 0
+    first_at = jnp.where(above_first, 3 * snps, snps)
+    width = band.shape[1]
+    units = snps // TILE
+
+    depth = 3
+
+    def copy_of(unit):
+        cut = pl.ds(pl.multiple_of(unit * TILE, TILE), TILE)
+        return pltpu.make_async_copy(band.at[cut], held.at[cut], sems.at[unit])
+
+    for unit in range(depth):
+        copy_of(unit).start()
+    extended[:, :snps] = jnp.zeros((rows, snps), jnp.float32)
+    extended[:, 2 * snps : 3 * snps] = own[...].astype(jnp.float32)
+    extended[:, 4 * snps :] = jnp.zeros((rows, snps + LANES), jnp.float32)
+    for at, piece in ((first_at, first), (4 * snps - first_at, second)):
+        extended[:, pl.ds(pl.multiple_of(at, LANES), snps)] = piece[...].astype(jnp.float32)
+
+    def per_unit(unit, carry):
+        start = starts[unit] + (2 - place) * snps
+        base = pl.multiple_of((start // LANES) * LANES, LANES)
+        window = window_tiles(extended, base, start - base, width // LANES)
+        copy_of(unit).wait()
+
+        @pl.when(unit + depth < units)
+        def _():
+            copy_of(unit + depth).start()
+
+        cut = pl.ds(pl.multiple_of(unit * TILE, TILE), TILE)
+        product[:, cut] = lax.dot_general(window, held[cut, :], NT, preferred_element_type=jnp.float32)
+        return carry
+
+    lax.fori_loop(0, units, per_unit, 0)
+
+
+def near_step(starts, own, first, second, band):
     rows, snps = own.shape
     width = band.shape[1]
-
-    @pl.when(unit == 0)
-    def _():
-        for at, piece in enumerate((far_below, below, own, above, far_above)):
-            extended[:, at * snps : (at + 1) * snps] = piece[...].astype(jnp.float32)
-        extended[:, 5 * snps :] = jnp.zeros((rows, LANES), jnp.float32)
-        square_acc[...] = jnp.zeros_like(square_acc)
-        count_acc[...] = jnp.zeros_like(count_acc)
-
-    start = starts[unit]
-    base = pl.multiple_of((start // LANES) * LANES, LANES)
-    shift = start - base
-    back = lax.rem(LANES - shift, LANES)
-    lane = lax.broadcasted_iota(jnp.int32, (rows, LANES), 1)
-    keep = lane < LANES - shift
-    window = []
-    turned = pltpu.roll(extended[:, pl.ds(base, LANES)], back, 1)
-    for at in range(width // LANES):
-        following = pltpu.roll(extended[:, pl.ds(base + (at + 1) * LANES, LANES)], back, 1)
-        window.append(jnp.where(keep, turned, following).astype(jnp.bfloat16))
-        turned = following
-    window = jnp.concatenate(window, axis=1)
-    product = lax.dot_general(window, band[...], NT, preferred_element_type=jnp.float32)
-
-    current = coef[...]
-    total = current + anc1[...].astype(jnp.float32) + anc2[...].astype(jnp.float32) + anc3[...].astype(jnp.float32)
-    gradient = current + product - targets[...] + merging * (current - total * (1.0 / ancestries))
-    value = current - step_size * gradient
-    proposal[...] = value
-    part = jnp.sum(value * value, axis=0, keepdims=True)
+    smem = pl.BlockSpec(memory_space=pltpu.SMEM)
+    vmem = pl.BlockSpec(memory_space=pltpu.VMEM)
+    return pl.pallas_call(
+        near_kernel,
+        in_specs=[smem, vmem, vmem, vmem, pl.BlockSpec(memory_space=pltpu.HBM)],
+        out_specs=[vmem, vmem],
+        out_shape=[
+            jax.ShapeDtypeStruct((rows, snps), jnp.float32),
+            jax.ShapeDtypeStruct(band.shape, band.dtype),
+        ],
+        scratch_shapes=[
+            pltpu.VMEM((rows, 5 * snps + LANES), jnp.float32),
+            pltpu.SemaphoreType.DMA((snps // TILE,)),
+        ],
+        compiler_params=pltpu.CompilerParams(vmem_limit_bytes=10 << 20),
+        cost_estimate=pl.CostEstimate(
+            flops=2 * rows * snps * width, bytes_accessed=2 * snps * width + 8 * rows * snps, transcendentals=0
+        ),
+        name="near_step",
+    )(starts, own, first, second, pltpu.with_memory_space_constraint(band, pltpu.HBM))
+
+
+def far_kernel(
+    ancestries, starts, first, second, held, product, coef, targets, core_copy, pair_copy, ids,
+    proposal, sums, far, square_acc, count_acc,
+):
+    rows, snps = coef.shape
+    units = snps // TILE
+    reach = 2 * TILE
+    place = place_of()
+    high_at = snps + 4 * TILE
+    first_at = jnp.where(lax.rem(place, 4) < 2, high_at, TILE)
+    far[:, snps - TILE :] = jnp.zeros((rows, far.shape[1] - snps + TILE), jnp.float32)
+    for at, piece in ((first_at, first), (high_at + TILE - first_at, second)):
+        far[:, pl.ds(pl.multiple_of(at, LANES), piece.shape[1])] = piece[...].astype(jnp.float32)
+    square_acc[...] = jnp.zeros_like(square_acc)
+    count_acc[...] = jnp.zeros_like(count_acc)
     group = lax.broadcasted_iota(jnp.int32, (GROUPS, LANES), 0)
-    squares = square_acc[...]
-    counts = count_acc[...]
-    for at in range(TILE // LANES):
-        here = ids[:, at * LANES : (at + 1) * LANES] == group
-        squares += jnp.where(here, part[:, at * LANES : (at + 1) * LANES], 0.0)
-        counts += jnp.where(here, 1.0, 0.0)
-    square_acc[...] = squares
-    count_acc[...] = counts
-
-    @pl.when(unit == pl.num_programs(0) - 1)
-    def _():
-        place = lax.broadcasted_iota(jnp.int32, (GROUPS, LANES), 1)
-        square_col = jnp.sum(squares, axis=1, keepdims=True)
-        count_col = jnp.sum(counts, axis=1, keepdims=True)
-        both = jnp.where(place == group, square_col, 0.0) + jnp.where(place == group + GROUPS, count_col * rows, 0.0)
-        sums[...] = jnp.broadcast_to(jnp.sum(both, axis=0, keepdims=True), sums.shape)
-
-
-def band_step(starts, pieces, band, coef, targets, ancs, ids, peers, ancestries):
+
+    def per_unit(unit, carry):
+        rows_from = pl.multiple_of(unit * TILE, TILE)
+        cut = pl.ds(rows_from, TILE)
+        start = starts[unit] + (2 - place) * snps
+        tiles = held.shape[1] // TILE
+        low_count = (jnp.maximum(snps - start, 0) + reach - 1) // reach
+        high_count = (jnp.maximum(start - 2 * snps, 0) + reach - 1) // reach
+        from_tile = jnp.where(high_count > 0, tiles - 2 * high_count, 0)
+        moved = start + jnp.where(high_count > 0, high_at - 4 * snps, 0)
+
+        def per_tile(step, total):
+            column = pl.multiple_of((from_tile + 2 * step) * TILE, TILE)
+            begin = moved + column
+            base = pl.multiple_of((begin // LANES) * LANES, LANES)
+            window = window_tiles(far, base, begin - base, reach // LANES)
+            return total + lax.dot_general(
+                window, held[cut, pl.ds(column, reach)], NT, preferred_element_type=jnp.float32
+            )
+
+        bands = lax.fori_loop(0, low_count + high_count, per_tile, product[:, cut])
+        current = coef[:, cut]
+        total = current + core_copy[:, cut].astype(jnp.float32) + pair_copy[:, cut].astype(jnp.float32)
+        gradient = current + bands - targets[:, cut] + merging * (current - total * (1.0 / ancestries))
+        value = current - step_size * gradient
+        proposal[:, cut] = value
+        part = jnp.sum(value * value, axis=0, keepdims=True)
+        ids_here = ids[:, cut]
+        squares = square_acc[...]
+        counts = count_acc[...]
+        for at in range(TILE // LANES):
+            here = ids_here[:, at * LANES : (at + 1) * LANES] == group
+            squares += jnp.where(here, part[:, at * LANES : (at + 1) * LANES], 0.0)
+            counts += jnp.where(here, 1.0, 0.0)
+        square_acc[...] = squares
+        count_acc[...] = counts
+        return carry
+
+    lax.fori_loop(0, units, per_unit, 0)
+    lane = lax.broadcasted_iota(jnp.int32, (GROUPS, LANES), 1)
+    square_col = jnp.sum(square_acc[...], axis=1, keepdims=True)
+    count_col = jnp.sum(count_acc[...], axis=1, keepdims=True)
+    both = jnp.where(lane == group, square_col, 0.0) + jnp.where(lane == group + GROUPS, count_col * rows, 0.0)
+    sums[...] = jnp.broadcast_to(jnp.sum(both, axis=0, keepdims=True), sums.shape)
+
+
+def far_step(starts, first, second, held, product, coef, targets, core_copy, pair_copy, ids, peers, ancestries):
     rows, snps = coef.shape
-    width = band.shape[1]
-    whole = pl.BlockSpec((rows, snps), lambda u: (0, 0))
-    tile = pl.BlockSpec((rows, TILE), lambda u: (0, u))
-    return pl.pallas_call(
-        functools.partial(band_kernel, ancestries),
-        grid=(snps // TILE,),
-        in_specs=[pl.BlockSpec(memory_space=pltpu.SMEM)]
-        + [whole] * 5
-        + [pl.BlockSpec((TILE, width), lambda u: (u, 0)), tile, tile, tile, tile, tile,
-           pl.BlockSpec((1, TILE), lambda u: (0, u))],
-        out_specs=[tile, pl.BlockSpec((peers, LANES), lambda u: (0, 0))],
+    smem = pl.BlockSpec(memory_space=pltpu.SMEM)
+    vmem = pl.BlockSpec(memory_space=pltpu.VMEM)
+    return pl.pallas_call(
+        functools.partial(far_kernel, ancestries),
+        in_specs=[smem] + [vmem] * 9,
+        out_specs=[vmem, vmem],
         out_shape=[
             jax.ShapeDtypeStruct((rows, snps), jnp.float32),
             jax.ShapeDtypeStruct((peers, LANES), jnp.float32),
         ],
         scratch_shapes=[
-            pltpu.VMEM((rows, 5 * snps + LANES), jnp.float32),
+            pltpu.VMEM((rows, 2 * snps + 4 * TILE + LANES), jnp.float32),
             pltpu.VMEM((GROUPS, LANES), jnp.float32),
             pltpu.VMEM((GROUPS, LANES), jnp.float32),
         ],
-        compiler_params=pltpu.CompilerParams(
-            dimension_semantics=("arbitrary",), vmem_limit_bytes=52 << 20
+        compiler_params=pltpu.CompilerParams(vmem_limit_bytes=10 << 20),
+        cost_estimate=pl.CostEstimate(
+            flops=2 * rows * snps * 1024, bytes_accessed=20 * rows * snps, transcendentals=0
         ),
-        cost_estimate=pl.CostEstimate(
-            flops=2 * rows * snps * width, bytes_accessed=2 * snps * width + 24 * rows * snps, transcendentals=0
-        ),
-        name="band_step",
-    )(starts, *pieces, band, coef, targets, *ancs, ids)
+        name="far_step",
+    )(starts, first, second, held, product, coef, targets, core_copy, pair_copy, ids)
 
 
 def score_kernel(scale, sums, weights, ids, proposal, dosage, updated, partial, low):
@@ -192,10 +292,10 @@
     )(arrived)
 
 
-def passed_along(block, axis, distance):
-    devices = range(lax.axis_size(axis))
-    route = [(i - distance, i) for i in devices if i - distance in devices]
-    return lax.ppermute(block, axis, route)
+def swapped(block, axis, distance, lower):
+    count = lax.axis_size(axis)
+    pairs = [(i, i + distance) for i in range(count - distance) if lower(i)]
+    return lax.ppermute(block, axis, pairs + [(j, i) for i, j in pairs])
 
 
 def per_device(coefficients, sumstats, linkage, band_start, group_ids, group_weight, dosage):
@@ -203,25 +303,21 @@
     targets = sumstats[0]
     band = linkage[0]
     starts = band_start[0]
-    snp_rows = current.shape[1]
     genome_count = lax.axis_size("genome")
     anc_count = lax.axis_size("anc")
-    position = lax.axis_index("genome")
-    low_copy = current.astype(jnp.bfloat16)
-    pieces = [
-        passed_along(low_copy, "genome", 2),
-        passed_along(low_copy, "genome", 1),
-        low_copy,
-        passed_along(low_copy, "genome", -1),
-        passed_along(low_copy, "genome", -2),
-    ]
-    ancs = [
-        lax.ppermute(low_copy, "anc", [(i, i ^ k) for i in range(anc_count)]) for k in range(1, anc_count)
-    ]
-    local_start = starts - position * snp_rows + 2 * snp_rows
+    low_copy, send_inside, send_across = cast_step(current)
+    far_inside = swapped(send_inside, "genome", 2, lambda i: i % 4 < 2)
+    far_across = swapped(send_across, "genome", 2, lambda i: i % 4 >= 2)
+    near_even = swapped(low_copy, "genome", 1, lambda i: i % 2 == 0)
+    near_odd = swapped(low_copy, "genome", 1, lambda i: i % 2 == 1)
+    core_copy = swapped(low_copy, "anc", 1, lambda i: i % 2 == 0)
+    pair_sum = (current + core_copy.astype(jnp.float32)).astype(jnp.bfloat16)
+    pair_copy = swapped(pair_sum, "anc", 2, lambda i: i < 2)
+    product, held = near_step(starts, low_copy, near_even, near_odd, band)
     peers = genome_count * lax.axis_size("trait")
-    proposal, sums = band_step(
-        local_start, pieces, band, current, targets, ancs, group_ids, peers, anc_count
+    proposal, sums = far_step(
+        starts, far_inside, far_across, held, product, current, targets, core_copy, pair_copy,
+        group_ids, peers, anc_count,
     )
     arrived = lax.all_to_all(
         sums.reshape(peers, 1, LANES), ("genome", "trait"), split_axis=0, concat_axis=0, tiled=True

time: 90.4 us -> 87.4 us (0.967)
  blocking collectives: 42.4 us -> 54.2 us
  waiting for transfers between devices: 10.2 us -> 0.02 us
  starting transfers between devices: 14 us -> 8.93 us
  Pallas kernels: 18.9 us -> 20.2 us
    all_to_all x1, blocking collectives: 27 us -> 38.8 us  [per_device(): lax.all_to_all(sums.reshape(peers, 1, LANES), ('genome', 'trait'), split_...]
    ppermute x7 -> x6, waiting for transfers between devices: 10.2 us -> 0.02 us  [swapped(): return lax.ppermute(block, axis, pairs + [(j, i) for i, j in pairs])]
    ppermute x7 -> x6, starting transfers between devices: 14 us -> 8.93 us  [swapped(): return lax.ppermute(block, axis, pairs + [(j, i) for i, j in pairs])]
    pallas_call x1 -> x3, Pallas kernels: 12.4 us -> 13.7 us  [the longest x1 10.1 us: near_step(): pl.pallas_call(near_kernel, in_specs=[smem, vmem, vmem, vmem, pl.BlockSpe...]
  transfers between devices with their start and end apart: 7 -> 6, of which waited for: 3 -> 0; matrix products, arithmetic and copies ran while one was open for 1% -> 1% of each run, Pallas kernels for 0% -> 12%
where the time goes in v2:
time: 87.4 us; the launch traced here: 86.8 us
  blocking collectives  54.2 us (62%)
  Pallas kernels  20.2 us (23%)
  starting transfers between devices  8.93 us (10%)
  local copies, waits for them, and re-layouts  1.63 us (2%)
  other arithmetic  1.11 us (1%)
    all_to_all x1, blocking collectives, per_device(): lax.all_to_all(sums.reshape(peers, 1, LANES), ('genome', 'trait'), split_...  38.8 us
    all_to_all x1, blocking collectives, per_device(): lax.all_to_all(partial, 'genome', split_axis=0, concat_axis=0, tiled=True)  15.4 us
    pallas_call x1, Pallas kernels, near_step(): pl.pallas_call(near_kernel, in_specs=[smem, vmem, vmem, vmem, pl.BlockSpe...  10.1 us
    ppermute x6, starting transfers between devices, swapped(): return lax.ppermute(block, axis, pairs + [(j, i) for i, j in pairs])  8.93 us
    pallas_call x1, Pallas kernels, score_step(): pl.pallas_call(functools.partial(score_kernel, 1.0 / math.sqrt(snps * gen...  4.83 us
    pallas_call x1, Pallas kernels, cast_step(): pl.pallas_call(cast_kernel, in_specs=[vmem], out_specs=[vmem] * 3, out_sh...  2.01 us
  transfers between devices with their start and end apart: 6, of which 0 were waited for; matrix products, arithmetic and copies ran while one was open for 1% of the time, Pallas kernels for 12%

profile of v2, /device:TPU:8, one launch (start us, length us, event | category | flops | bytes accessed | tf_op | source)
XLA Modules:
  0.0 86.8 jit_solution(17967161239626716376)
XLA Ops:
  0.6 0.0 copy-start
  0.7 2.0 %cast_step.1 = (bf16[64,2048]{1,0:T(8,128)(2,1)}, bf16[64,1792]{1,0:T(8,128)(2,1)}, bf16[64,1792]{1,0:T(8,128)(2,1)}) custom-call(f32[64,2048]{1,0:T(8,128)} %bitcast.15), custom_call_target="tpu_custom_call" | custom-call | tf_op jit(solution)/shard_map/cast_step/pallas_call | solution.py:37
  2.7 0.0 collective-permute-start.4
  2.7 1.5 %collective-permute-start.2 = (bf16[64,2048]{1,0:T(8,128)(2,1)}, bf16[64,2048]{1,0:T(8,128)(2,1)S(1)}, u32[]{:S(2)}, u32[]{:S(2)}) collective-permute-start(bf16[64,2048]{1,0:T(8,128)(2,1)} %get-tuple-element.13.own), channel_id=1, source_target_pairs={{0,8},{16,24},{32,40},{48,56},{64,72},{80,88},{96,104},{112,120},{... | collective-permute-start | bytes 786440 | tf_op jit(solution)/shard_map/ppermute | solution.py:298
  4.2 0.7 collective-permute-start.3
  4.8 0.0 collective-permute-done.4.core_copy
  4.9 1.1 %add_convert_fusion = bf16[64,2048]{1,0:T(8,128)(2,1)S(1)} fusion(bf16[64,2048]{1,0:T(8,128)(2,1)S(1)} %collective-permute-done.4.core_copy, f32[1,64,2048]{2,1,0:T(8,128)} %param.7), kind=kLoop, calls=%fused_computation | loop fusion | flops 393216 | bytes 1048576 | tf_op jit(solution)/shard_map/convert_element_type | solution.py:314
  6.0 1.8 %collective-permute-start.5 = (bf16[64,2048]{1,0:T(8,128)(2,1)S(1)}, bf16[64,2048]{1,0:T(8,128)(2,1)S(1)}, u32[]{:S(2)}, u32[]{:S(2)}) collective-permute-start(bf16[64,2048]{1,0:T(8,128)(2,1)S(1)} %add_convert_fusion), channel_id=1, source_target_pairs={{0,4},{2,6},{4,0},{6,2},{1,5},{3,7},{5,1},{7,3},{8,12},{10,14},{12... | collective-permute-start | bytes 786440 | tf_op jit(solution)/shard_map/ppermute | solution.py:298
  7.8 4.3 %collective-permute-start = (bf16[64,1792]{1,0:T(8,128)(2,1)}, bf16[64,1792]{1,0:T(8,128)(2,1)S(1)}, u32[]{:S(2)}, u32[]{:S(2)}) collective-permute-start(bf16[64,1792]{1,0:T(8,128)(2,1)} %get-tuple-element.11), channel_id=1, source_target_pairs={{0,16},{8,24},{32,48},{40,56},{64,80},{72,88},{96,112},{104,120},{... | collective-permute-start | bytes 688136 | tf_op jit(solution)/shard_map/ppermute | solution.py:298
  12.1 0.7 collective-permute-start.1
  12.7 0.0 collective-permute-done.2.first
  12.8 0.0 collective-permute-done.3.second
  12.8 0.0 copy-start.2
  12.8 0.9 %copy-done.2 = bf16[64,2048]{1,0:T(8,128)(2,1)S(1)} copy-done((bf16[64,2048]{1,0:T(8,128)(2,1)S(1)}, bf16[64,2048]{1,0:T(8,128)(2,1)}, u32[]{:S(2)}) %copy-start.2) | copy-done | bytes 262168
  13.7 0.7 copy-done.4
  14.4 10.1 %near_step.1 = (f32[64,2048]{1,0:T(8,128)S(1)}, bf16[2048,4096]{1,0:T(8,128)(2,1)S(1)}) custom-call(s32[8]{0:T(128)S(1)} %bitcast.20, bf16[64,2048]{1,0:T(8,128)(2,1)S(1)} %copy-done.2, bf16[64,2048]{1,0:T(8,128)(2,1)S(1)} %collective-permute-done.2.first, bf16[64,2048]{1,0:T(8,128)(2,1)S(1)} %collective-permute-done.3.second, bf16[2048,4096]{1,0:T(8,128)(2,1)} %bitcast.22), custom_call_target="tpu_custom_call" | custom-call | flops 1073741824 | bytes 17825792 | tf_op jit(solution)/shard_map/near_step/pallas_call | solution.py:103
  24.5 0.0 collective-permute-done.first
  24.5 0.0 collective-permute-done.5.pair_copy
  24.5 0.0 slice-start.1
  24.5 1.6 %far_step.1 = (f32[64,2048]{1,0:T(8,128)S(1)}, f32[64,128]{1,0:T(8,128)S(1)}) custom-call(s32[8]{0:T(128)S(1)} %bitcast.21, bf16[64,1792]{1,0:T(8,128)(2,1)S(1)} %collective-permute-done.first, bf16[64,1792]{1,0:T(8,128)(2,1)S(1)} %collective-permute-done.1.second, bf16[2048,4096]{1,0:T(8,128)(2,1)S(1)} %get-tuple-element.14.held, ...), custom_call_target="tpu_custom_call" | custom-call | flops 268435456 | bytes 2621440 | tf_op jit(solution)/shard_map/far_step/pallas_call | solution.py:189
  26.1 38.8 %all_to_all.10 = f32[64,1,128]{2,1,0:T(1,128)S(1)} all-to-all(f32[64,1,128]{2,1,0:T(1,128)S(1)} %bitcast.19), channel_id=1, replica_groups=mesh['genome'=32,'anc'=4,'trait'=2] {'genome','trait'}, dimensions={0} | all-to-all | bytes 65536 | tf_op jit(solution)/shard_map/all_to_all | solution.py:322
  64.9 4.8 %score_step.1 = (f32[64,2048]{1,0:T(8,128)}, bf16[32,32,128]{2,1,0:T(8,128)(2,1)S(1)}) custom-call(f32[64,128]{1,0:T(8,128)S(1)} %bitcast.18, f32[1,64]{1,0:T(1,128)S(1)} %copy-done.5, s32[1,2048]{1,0:T(1,128)S(1)} %copy-done.3, f32[64,2048]{1,0:T(8,128)S(1)} %get-tuple-element.17.proposal, bf16[2048,2048]{1,0:T(8,128)(2,1)S(1)} %bitcast.14), custom_call_target="tpu_custom_call" | custom-call | flops 536870912 | bytes 9437184 | tf_op jit(solution)/shard_map/score_step/pallas_call | solution.py:252
  69.8 15.4 %all_to_all.11.arrived = bf16[32,32,128]{2,1,0:T(8,128)(2,1)} all-to-all(bf16[32,32,128]{2,1,0:T(8,128)(2,1)S(1)} %get-tuple-element.19), channel_id=1, replica_groups=mesh['genome'=32,'anc'=4,'trait'=2] {'genome'}, dimensions={0} | all-to-all | bytes 524288 | tf_op jit(solution)/shard_map/all_to_all | solution.py:326
  85.1 1.7 %total_step.1 = f32[64,64]{1,0:T(8,128)} custom-call(bf16[32,32,128]{2,1,0:T(8,128)(2,1)} %all_to_all.11.arrived), custom_call_target="tpu_custom_call" | custom-call | tf_op jit(solution)/shard_map/total_step/pallas_call | solution.py:288
  (13 shorter events, 0.0 us)
Async XLA Ops:
  0.6 23.9 %copy-start = (f32[1,64,2048]{2,1,0:T(8,128)S(1)}, f32[1,64,2048]{2,1,0:T(8,128)}, u32[]{:S(2)}) copy-start(f32[1,64,2048]{2,1,0:T(8,128)} %param.7) | copy-start | bytes 1572868
  0.6 23.9 %copy-start.1 = (f32[1,64,2048]{2,1,0:T(8,128)S(1)}, f32[1,64,2048]{2,1,0:T(8,128)}, u32[]{:S(2)}) copy-start(f32[1,64,2048]{2,1,0:T(8,128)} %param.8) | copy-start | bytes 1572868
  0.7 23.9 %copy-start.3 = (s32[1,2048]{1,0:T(1,128)S(1)}, s32[1,2048]{1,0:T(1,128)}, u32[]{:S(2)}) copy-start(s32[1,2048]{1,0:T(1,128)} %ids.3) | copy-start | bytes 24580
  2.7 2.2 %collective-permute-start.4 = (bf16[64,2048]{1,0:T(8,128)(2,1)}, bf16[64,2048]{1,0:T(8,128)(2,1)S(1)}, u32[]{:S(2)}, u32[]{:S(2)}) collective-permute-start(bf16[64,2048]{1,0:T(8,128)(2,1)} %get-tuple-element.13.own), channel_id=1, source_target_pairs={{0,2},{4,6},{2,0},{6,4},{1,3},{5,7},{3,1},{7,5},{8,10},{12,14},{10... | collective-permute-start | bytes 786440 | tf_op jit(solution)/shard_map/ppermute | solution.py:298
  2.7 10.1 %collective-permute-start.2 = (bf16[64,2048]{1,0:T(8,128)(2,1)}, bf16[64,2048]{1,0:T(8,128)(2,1)S(1)}, u32[]{:S(2)}, u32[]{:S(2)}) collective-permute-start(bf16[64,2048]{1,0:T(8,128)(2,1)} %get-tuple-element.13.own), channel_id=1, source_target_pairs={{0,8},{16,24},{32,40},{48,56},{64,72},{80,88},{96,104},{112,120},{... | collective-permute-start | bytes 786440 | tf_op jit(solution)/shard_map/ppermute | solution.py:298
  4.2 8.6 %collective-permute-start.3 = (bf16[64,2048]{1,0:T(8,128)(2,1)}, bf16[64,2048]{1,0:T(8,128)(2,1)S(1)}, u32[]{:S(2)}, u32[]{:S(2)}) collective-permute-start(bf16[64,2048]{1,0:T(8,128)(2,1)} %get-tuple-element.13.own), channel_id=1, source_target_pairs={{8,16},{24,32},{40,48},{56,64},{72,80},{88,96},{104,112},{120,128}... | collective-permute-start | bytes 786440 | tf_op jit(solution)/shard_map/ppermute | solution.py:298
  6.0 18.5 %collective-permute-start.5 = (bf16[64,2048]{1,0:T(8,128)(2,1)S(1)}, bf16[64,2048]{1,0:T(8,128)(2,1)S(1)}, u32[]{:S(2)}, u32[]{:S(2)}) collective-permute-start(bf16[64,2048]{1,0:T(8,128)(2,1)S(1)} %add_convert_fusion), channel_id=1, source_target_pairs={{0,4},{2,6},{4,0},{6,2},{1,5},{3,7},{5,1},{7,3},{8,12},{10,14},{12... | collective-permute-start | bytes 786440 | tf_op jit(solution)/shard_map/ppermute | solution.py:298
  7.8 16.7 %collective-permute-start = (bf16[64,1792]{1,0:T(8,128)(2,1)}, bf16[64,1792]{1,0:T(8,128)(2,1)S(1)}, u32[]{:S(2)}, u32[]{:S(2)}) collective-permute-start(bf16[64,1792]{1,0:T(8,128)(2,1)} %get-tuple-element.11), channel_id=1, source_target_pairs={{0,16},{8,24},{32,48},{40,56},{64,80},{72,88},{96,112},{104,120},{... | collective-permute-start | bytes 688136 | tf_op jit(solution)/shard_map/ppermute | solution.py:298
  12.1 12.4 %collective-permute-start.1 = (bf16[64,1792]{1,0:T(8,128)(2,1)}, bf16[64,1792]{1,0:T(8,128)(2,1)S(1)}, u32[]{:S(2)}, u32[]{:S(2)}) collective-permute-start(bf16[64,1792]{1,0:T(8,128)(2,1)} %get-tuple-element.12), channel_id=1, source_target_pairs={{16,32},{24,40},{48,64},{56,72},{80,96},{88,104},{112,128},{120,13... | collective-permute-start | bytes 688136 | tf_op jit(solution)/shard_map/ppermute | solution.py:298
  12.8 1.0 %copy-start.2 = (bf16[64,2048]{1,0:T(8,128)(2,1)S(1)}, bf16[64,2048]{1,0:T(8,128)(2,1)}, u32[]{:S(2)}) copy-start(bf16[64,2048]{1,0:T(8,128)(2,1)} %get-tuple-element.13.own) | copy-start | bytes 786436
  13.7 0.7 copy-start.4
  14.4 50.5 %slice-start = ((s8[8388608]{0:T(1024)(128)(4,1)}), s8[4194304]{0:T(1024)(128)(4,1)S(1)}, s32[]{:S(2)}) async-start(s8[8388608]{0:T(1024)(128)(4,1)} %bitcast.12), calls=%async_computation.2 | async-start | bytes 8388608
  14.4 50.5 %copy-start.5 = (f32[1,64]{1,0:T(1,128)S(1)}, f32[1,64]{1,0:T(1,128)}, u32[]{:S(2)}) copy-start(f32[1,64]{1,0:T(1,128)} %weights.1) | copy-start | bytes 772
  24.5 40.4 %slice-start.1 = ((s8[8388608]{0:T(1024)(128)(4,1)}), s8[4194304]{0:T(1024)(128)(4,1)S(1)}, s32[]{:S(2)}) async-start(s8[8388608]{0:T(1024)(128)(4,1)} %bitcast.12), calls=%async_computation.3 | async-start | bytes 8388608

commit v3 on v2

--- a/solution.py
+++ b/solution.py
@@ -21,26 +21,6 @@
 
 def place_of():
     return lax.axis_index("genome")
-
-
-def cast_kernel(coef, low, first, second):
-    skip = jnp.where(lax.rem(place_of(), 4) < 2, TILE, 0)
-    low[...] = coef[...].astype(jnp.bfloat16)
-    for begin, out in ((skip, first), (TILE - skip, second)):
-        out[...] = coef[:, pl.ds(pl.multiple_of(begin, TILE), out.shape[1])].astype(jnp.bfloat16)
-
-
-def cast_step(coef):
-    rows, snps = coef.shape
-    part = jax.ShapeDtypeStruct((rows, snps - TILE), jnp.bfloat16)
-    vmem = pl.BlockSpec(memory_space=pltpu.VMEM)
-    return pl.pallas_call(
-        cast_kernel,
-        in_specs=[vmem],
-        out_specs=[vmem] * 3,
-        out_shape=[jax.ShapeDtypeStruct((rows, snps), jnp.bfloat16), part, part],
-        name="cast_step",
-    )(coef)
 
 
 def window_tiles(source, base, shift, count):
@@ -56,7 +36,7 @@
     return jnp.concatenate(tiles, axis=1)
 
 
-def near_kernel(starts, own, first, second, band, product, held, extended, sems):
+def near_kernel(starts_in, own, first, second, band, product, held, extended, starts, sems, start_sem):
     rows, snps = own.shape
     place = place_of()
     above_first = lax.rem(place, 2) == 0
@@ -70,6 +50,8 @@
         cut = pl.ds(pl.multiple_of(unit * TILE, TILE), TILE)
         return pltpu.make_async_copy(band.at[cut], held.at[cut], sems.at[unit])
 
+    start_copy = pltpu.make_async_copy(starts_in, starts, start_sem)
+    start_copy.start()
     for unit in range(depth):
         copy_of(unit).start()
     extended[:, :snps] = jnp.zeros((rows, snps), jnp.float32)
@@ -77,9 +59,10 @@
     extended[:, 4 * snps :] = jnp.zeros((rows, snps + LANES), jnp.float32)
     for at, piece in ((first_at, first), (4 * snps - first_at, second)):
         extended[:, pl.ds(pl.multiple_of(at, LANES), snps)] = piece[...].astype(jnp.float32)
+    start_copy.wait()
 
     def per_unit(unit, carry):
-        start = starts[unit] + (2 - place) * snps
+        start = starts[0, unit] + (2 - place) * snps
         base = pl.multiple_of((start // LANES) * LANES, LANES)
         window = window_tiles(extended, base, start - base, width // LANES)
         copy_of(unit).wait()
@@ -98,11 +81,11 @@
 def near_step(starts, own, first, second, band):
     rows, snps = own.shape
     width = band.shape[1]
-    smem = pl.BlockSpec(memory_space=pltpu.SMEM)
+    hbm = pl.BlockSpec(memory_space=pltpu.HBM)
     vmem = pl.BlockSpec(memory_space=pltpu.VMEM)
     return pl.pallas_call(
         near_kernel,
-        in_specs=[smem, vmem, vmem, vmem, pl.BlockSpec(memory_space=pltpu.HBM)],
+        in_specs=[hbm, vmem, vmem, vmem, hbm],
         out_specs=[vmem, vmem],
         out_shape=[
             jax.ShapeDtypeStruct((rows, snps), jnp.float32),
@@ -110,37 +93,46 @@
         ],
         scratch_shapes=[
             pltpu.VMEM((rows, 5 * snps + LANES), jnp.float32),
+            pltpu.SMEM((1, snps // TILE), jnp.int32),
             pltpu.SemaphoreType.DMA((snps // TILE,)),
+            pltpu.SemaphoreType.DMA,
         ],
         compiler_params=pltpu.CompilerParams(vmem_limit_bytes=10 << 20),
         cost_estimate=pl.CostEstimate(
             flops=2 * rows * snps * width, bytes_accessed=2 * snps * width + 8 * rows * snps, transcendentals=0
         ),
         name="near_step",
-    )(starts, own, first, second, pltpu.with_memory_space_constraint(band, pltpu.HBM))
+    )(
+        pltpu.with_memory_space_constraint(starts, pltpu.HBM), own, first, second,
+        pltpu.with_memory_space_constraint(band, pltpu.HBM),
+    )
 
 
 def far_kernel(
-    ancestries, starts, first, second, held, product, coef, targets, core_copy, pair_copy, ids,
-    proposal, sums, far, square_acc, count_acc,
+    ancestries, starts_in, first, second, held, product, coef, targets, core_copy, pair_copy, ids,
+    proposal, sums, far, square_acc, count_acc, starts, start_sem,
 ):
     rows, snps = coef.shape
     units = snps // TILE
     reach = 2 * TILE
     place = place_of()
     high_at = snps + 4 * TILE
-    first_at = jnp.where(lax.rem(place, 4) < 2, high_at, TILE)
-    far[:, snps - TILE :] = jnp.zeros((rows, far.shape[1] - snps + TILE), jnp.float32)
-    for at, piece in ((first_at, first), (high_at + TILE - first_at, second)):
+    first_at = jnp.where(lax.rem(place, 2) == 0, high_at, 0)
+    start_copy = pltpu.make_async_copy(starts_in, starts, start_sem)
+    start_copy.start()
+    far[:, snps:high_at] = jnp.zeros((rows, high_at - snps), jnp.float32)
+    far[:, high_at + snps :] = jnp.zeros((rows, LANES), jnp.float32)
+    for at, piece in ((first_at, first), (high_at - first_at, second)):
         far[:, pl.ds(pl.multiple_of(at, LANES), piece.shape[1])] = piece[...].astype(jnp.float32)
     square_acc[...] = jnp.zeros_like(square_acc)
     count_acc[...] = jnp.zeros_like(count_acc)
+    start_copy.wait()
     group = lax.broadcasted_iota(jnp.int32, (GROUPS, LANES), 0)
 
     def per_unit(unit, carry):
         rows_from = pl.multiple_of(unit * TILE, TILE)
         cut = pl.ds(rows_from, TILE)
-        start = starts[unit] + (2 - place) * snps
+        start = starts[0, unit] + (2 - place) * snps
         tiles = held.shape[1] // TILE
         low_count = (jnp.maximum(snps - start, 0) + reach - 1) // reach
         high_count = (jnp.maximum(start - 2 * snps, 0) + reach - 1) // reach
@@ -184,11 +176,11 @@
 
 def far_step(starts, first, second, held, product, coef, targets, core_copy, pair_copy, ids, peers, ancestries):
     rows, snps = coef.shape
-    smem = pl.BlockSpec(memory_space=pltpu.SMEM)
+    hbm = pl.BlockSpec(memory_space=pltpu.HBM)
     vmem = pl.BlockSpec(memory_space=pltpu.VMEM)
     return pl.pallas_call(
         functools.partial(far_kernel, ancestries),
-        in_specs=[smem] + [vmem] * 9,
+        in_specs=[hbm] + [vmem] * 9,
         out_specs=[vmem, vmem],
         out_shape=[
             jax.ShapeDtypeStruct((rows, snps), jnp.float32),
@@ -198,13 +190,17 @@
             pltpu.VMEM((rows, 2 * snps + 4 * TILE + LANES), jnp.float32),
             pltpu.VMEM((GROUPS, LANES), jnp.float32),
             pltpu.VMEM((GROUPS, LANES), jnp.float32),
+            pltpu.SMEM((1, snps // TILE), jnp.int32),
+            pltpu.SemaphoreType.DMA,
         ],
         compiler_params=pltpu.CompilerParams(vmem_limit_bytes=10 << 20),
         cost_estimate=pl.CostEstimate(
             flops=2 * rows * snps * 1024, bytes_accessed=20 * rows * snps, transcendentals=0
         ),
         name="far_step",
-    )(starts, first, second, held, product, coef, targets, core_copy, pair_copy, ids)
+    )(
+        pltpu.with_memory_space_constraint(starts, pltpu.HBM), first, second, held, product, coef, targets, core_copy, pair_copy, ids,
+    )
 
 
 def score_kernel(scale, sums, weights, ids, proposal, dosage, updated, partial, low):
@@ -302,21 +298,20 @@
     current = coefficients[0]
     targets = sumstats[0]
     band = linkage[0]
-    starts = band_start[0]
     genome_count = lax.axis_size("genome")
     anc_count = lax.axis_size("anc")
-    low_copy, send_inside, send_across = cast_step(current)
-    far_inside = swapped(send_inside, "genome", 2, lambda i: i % 4 < 2)
-    far_across = swapped(send_across, "genome", 2, lambda i: i % 4 >= 2)
+    low_copy = current.astype(jnp.bfloat16)
     near_even = swapped(low_copy, "genome", 1, lambda i: i % 2 == 0)
     near_odd = swapped(low_copy, "genome", 1, lambda i: i % 2 == 1)
+    far_even = swapped(near_odd, "genome", 1, lambda i: i % 2 == 0)
+    far_odd = swapped(near_even, "genome", 1, lambda i: i % 2 == 1)
     core_copy = swapped(low_copy, "anc", 1, lambda i: i % 2 == 0)
     pair_sum = (current + core_copy.astype(jnp.float32)).astype(jnp.bfloat16)
     pair_copy = swapped(pair_sum, "anc", 2, lambda i: i < 2)
-    product, held = near_step(starts, low_copy, near_even, near_odd, band)
+    product, held = near_step(band_start, low_copy, near_even, near_odd, band)
     peers = genome_count * lax.axis_size("trait")
     proposal, sums = far_step(
-        starts, far_inside, far_across, held, product, current, targets, core_copy, pair_copy,
+        band_start, far_even, far_odd, held, product, current, targets, core_copy, pair_copy,
         group_ids, peers, anc_count,
     )
     arrived = lax.all_to_all(

time: 87.4 us -> 80 us (0.915)
  blocking collectives: 54.2 us -> 46 us
  starting transfers between devices: 8.93 us -> 11.7 us
  Pallas kernels: 20.2 us -> 18.3 us
  local copies, waits for them, and re-layouts: 1.63 us -> 0.04 us
  other arithmetic: 1.11 us -> 2.26 us
    all_to_all x1, blocking collectives: 38.8 us -> 30.5 us  [per_device(): lax.all_to_all(sums.reshape(peers, 1, LANES), ('genome', 'trait'), split_...]
    ppermute x6, starting transfers between devices: 8.93 us -> 11.7 us  [swapped(): return lax.ppermute(block, axis, pairs + [(j, i) for i, j in pairs])]
    pallas_call x3 -> x2, Pallas kernels: 13.7 us -> 11.8 us  [the longest x1 9.44 us: near_step(): pl.pallas_call(near_kernel, in_specs=[hbm, vmem, vmem, vmem, hbm], out_sp...]
    unnamed x16 -> x12, local copies, waits for them, and re-layouts: 1.63 us -> 0.04 us
    convert_element_type x0 -> x1, other arithmetic: none -> 1.15 us  [per_device(): low_copy = current.astype(jnp.bfloat16)]
where the time goes in v3:
time: 80 us; the launch traced here: 79.1 us
  blocking collectives  46 us (58%)
  Pallas kernels  18.3 us (23%)
  starting transfers between devices  11.7 us (15%)
  other arithmetic  2.26 us (3%)
    all_to_all x1, blocking collectives, per_device(): lax.all_to_all(sums.reshape(peers, 1, LANES), ('genome', 'trait'), split_...  30.5 us
    all_to_all x1, blocking collectives, per_device(): lax.all_to_all(partial, 'genome', split_axis=0, concat_axis=0, tiled=True)  15.5 us
    ppermute x6, starting transfers between devices, swapped(): return lax.ppermute(block, axis, pairs + [(j, i) for i, j in pairs])  11.7 us
    pallas_call x1, Pallas kernels, near_step(): pl.pallas_call(near_kernel, in_specs=[hbm, vmem, vmem, vmem, hbm], out_sp...  9.44 us
    pallas_call x1, Pallas kernels, score_step(): pl.pallas_call(functools.partial(score_kernel, 1.0 / math.sqrt(snps * gen...  4.82 us
    pallas_call x1, Pallas kernels, far_step(): pl.pallas_call(functools.partial(far_kernel, ancestries), in_specs=[hbm]...  2.4 us
    pallas_call x1, Pallas kernels, total_step(): pl.pallas_call(total_kernel, out_shape=jax.ShapeDtypeStruct((rows, LANES...  1.68 us
  transfers between devices with their start and end apart: 6, of which 0 were waited for; matrix products, arithmetic and copies ran while one was open for 1% of the time, Pallas kernels for 12%

profile of v3, /device:TPU:8, one launch (start us, length us, event | category | flops | bytes accessed | tf_op | source)
XLA Modules:
  0.0 79.1 jit_solution(16527422213323568050)
XLA Ops:
  0.6 0.0 copy-start
  0.7 1.2 %bitcast_convert_fusion.own = bf16[64,2048]{1,0:T(8,128)(2,1)S(1)} fusion(f32[1,64,2048]{2,1,0:T(8,128)} %param.7), kind=kLoop, calls=%fused_computation.1 | loop fusion | flops 131072 | bytes 786432 | tf_op jit(solution)/shard_map/convert_element_type | solution.py:303
  1.8 0.1 collective-permute-start.4
  1.9 0.7 collective-permute-start
  2.6 4.3 %collective-permute-start.2 = (bf16[64,2048]{1,0:T(8,128)(2,1)S(1)}, bf16[64,2048]{1,0:T(8,128)(2,1)S(1)}, u32[]{:S(2)}, u32[]{:S(2)}) collective-permute-start(bf16[64,2048]{1,0:T(8,128)(2,1)S(1)} %bitcast_convert_fusion.own), channel_id=1, source_target_pairs={{0,8},{16,24},{32,40},{48,56},{64,72},{80,88},{96,104},{112,120},{... | collective-permute-start | bytes 786440 | tf_op jit(solution)/shard_map/ppermute | solution.py:294
  6.9 0.0 collective-permute-done.4.core_copy
  6.9 1.1 %add_convert_fusion = bf16[64,2048]{1,0:T(8,128)(2,1)S(1)} fusion(bf16[64,2048]{1,0:T(8,128)(2,1)S(1)} %collective-permute-done.4.core_copy, f32[1,64,2048]{2,1,0:T(8,128)} %param.7), kind=kLoop, calls=%fused_computation | loop fusion | flops 393216 | bytes 1048576 | tf_op jit(solution)/shard_map/convert_element_type | solution.py:309
  8.0 0.5 collective-permute-start.5
  8.6 0.0 collective-permute-done.second
  8.6 5.4 %collective-permute-start.1 = (bf16[64,2048]{1,0:T(8,128)(2,1)S(1)}, bf16[64,2048]{1,0:T(8,128)(2,1)S(1)}, u32[]{:S(2)}, u32[]{:S(2)}) collective-permute-start(bf16[64,2048]{1,0:T(8,128)(2,1)S(1)} %collective-permute-done.second), channel_id=1, source_target_pairs={{0,8},{16,24},{32,40},{48,56},{64,72},{80,88},{96,104},{112,120},{... | collective-permute-start | bytes 786440 | tf_op jit(solution)/shard_map/ppermute | solution.py:294
  14.0 0.0 collective-permute-done.2.first
  14.0 0.7 collective-permute-start.3
  14.7 0.0 slice-start
  14.7 0.0 copy-start.3
  14.7 9.4 %near_step.1 = (f32[64,2048]{1,0:T(8,128)S(1)}, bf16[2048,4096]{1,0:T(8,128)(2,1)S(1)}) custom-call(s32[1,8]{1,0:T(1,128)} %starts_in.3, bf16[64,2048]{1,0:T(8,128)(2,1)S(1)} %bitcast_convert_fusion.own, bf16[64,2048]{1,0:T(8,128)(2,1)S(1)} %collective-permute-done.2.first, bf16[64,2048]{1,0:T(8,128)(2,1)S(1)} %collective-permute-done.second, ...), custom_call_target="tpu_custom_call" | custom-call | flops 1073741824 | bytes 17825792 | tf_op jit(solution)/shard_map/near_step/pallas_call | solution.py:86
  24.1 0.0 collective-permute-done.5.pair_copy
  24.2 0.0 collective-permute-done.1.first
  24.2 0.0 collective-permute-done.3.second
  24.2 0.0 slice-start.1
  24.2 2.4 %far_step.1 = (f32[64,2048]{1,0:T(8,128)S(1)}, f32[64,128]{1,0:T(8,128)S(1)}) custom-call(s32[1,8]{1,0:T(1,128)} %starts_in.3, bf16[64,2048]{1,0:T(8,128)(2,1)S(1)} %collective-permute-done.1.first, bf16[64,2048]{1,0:T(8,128)(2,1)S(1)} %collective-permute-done.3.second, bf16[2048,4096]{1,0:T(8,128)(2,1)S(1)} %get-tuple-element.8.held, ...), custom_call_target="tpu_custom_call" | custom-call | flops 268435456 | bytes 2621440 | tf_op jit(solution)/shard_map/far_step/pallas_call | solution.py:181
  26.6 30.5 %all_to_all.10 = f32[64,1,128]{2,1,0:T(1,128)S(1)} all-to-all(f32[64,1,128]{2,1,0:T(1,128)S(1)} %bitcast.18), channel_id=1, replica_groups=mesh['genome'=32,'anc'=4,'trait'=2] {'genome','trait'}, dimensions={0} | all-to-all | bytes 65536 | tf_op jit(solution)/shard_map/all_to_all | solution.py:317
  57.1 4.8 %score_step.1 = (f32[64,2048]{1,0:T(8,128)}, bf16[32,32,128]{2,1,0:T(8,128)(2,1)S(1)}) custom-call(f32[64,128]{1,0:T(8,128)S(1)} %bitcast.17, f32[1,64]{1,0:T(1,128)S(1)} %copy-done.3, s32[1,2048]{1,0:T(1,128)S(1)} %copy-done.2, f32[64,2048]{1,0:T(8,128)S(1)} %get-tuple-element.11.proposal, bf16[2048,2048]{1,0:T(8,128)(2,1)S(1)} %bitcast.14), custom_call_target="tpu_custom_call" | custom-call | flops 536870912 | bytes 9437184 | tf_op jit(solution)/shard_map/score_step/pallas_call | solution.py:248
  62.0 15.5 %all_to_all.11.arrived = bf16[32,32,128]{2,1,0:T(8,128)(2,1)} all-to-all(bf16[32,32,128]{2,1,0:T(8,128)(2,1)S(1)} %get-tuple-element.13), channel_id=1, replica_groups=mesh['genome'=32,'anc'=4,'trait'=2] {'genome'}, dimensions={0} | all-to-all | bytes 524288 | tf_op jit(solution)/shard_map/all_to_all | solution.py:321
  77.4 1.7 %total_step.1 = f32[64,64]{1,0:T(8,128)} custom-call(bf16[32,32,128]{2,1,0:T(8,128)(2,1)} %all_to_all.11.arrived), custom_call_target="tpu_custom_call" | custom-call | tf_op jit(solution)/shard_map/total_step/pallas_call | solution.py:284
  (9 shorter events, 0.0 us)
Async XLA Ops:
  0.6 23.6 %copy-start = (f32[1,64,2048]{2,1,0:T(8,128)S(1)}, f32[1,64,2048]{2,1,0:T(8,128)}, u32[]{:S(2)}) copy-start(f32[1,64,2048]{2,1,0:T(8,128)} %param.7) | copy-start | bytes 1572868
  0.6 23.6 %copy-start.1 = (f32[1,64,2048]{2,1,0:T(8,128)S(1)}, f32[1,64,2048]{2,1,0:T(8,128)}, u32[]{:S(2)}) copy-start(f32[1,64,2048]{2,1,0:T(8,128)} %param.8) | copy-start | bytes 1572868
  0.7 23.6 %copy-start.2 = (s32[1,2048]{1,0:T(1,128)S(1)}, s32[1,2048]{1,0:T(1,128)}, u32[]{:S(2)}) copy-start(s32[1,2048]{1,0:T(1,128)} %ids.3) | copy-start | bytes 24580
  1.8 5.1 %collective-permute-start.4 = (bf16[64,2048]{1,0:T(8,128)(2,1)S(1)}, bf16[64,2048]{1,0:T(8,128)(2,1)S(1)}, u32[]{:S(2)}, u32[]{:S(2)}) collective-permute-start(bf16[64,2048]{1,0:T(8,128)(2,1)S(1)} %bitcast_convert_fusion.own), channel_id=1, source_target_pairs={{0,2},{4,6},{2,0},{6,4},{1,3},{5,7},{3,1},{7,5},{8,10},{12,14},{10... | collective-permute-start | bytes 786440 | tf_op jit(solution)/shard_map/ppermute | solution.py:294
  1.9 6.6 %collective-permute-start = (bf16[64,2048]{1,0:T(8,128)(2,1)S(1)}, bf16[64,2048]{1,0:T(8,128)(2,1)S(1)}, u32[]{:S(2)}, u32[]{:S(2)}) collective-permute-start(bf16[64,2048]{1,0:T(8,128)(2,1)S(1)} %bitcast_convert_fusion.own), channel_id=1, source_target_pairs={{8,16},{24,32},{40,48},{56,64},{72,80},{88,96},{104,112},{120,128}... | collective-permute-start | bytes 786440 | tf_op jit(solution)/shard_map/ppermute | solution.py:294
  2.6 11.4 %collective-permute-start.2 = (bf16[64,2048]{1,0:T(8,128)(2,1)S(1)}, bf16[64,2048]{1,0:T(8,128)(2,1)S(1)}, u32[]{:S(2)}, u32[]{:S(2)}) collective-permute-start(bf16[64,2048]{1,0:T(8,128)(2,1)S(1)} %bitcast_convert_fusion.own), channel_id=1, source_target_pairs={{0,8},{16,24},{32,40},{48,56},{64,72},{80,88},{96,104},{112,120},{... | collective-permute-start | bytes 786440 | tf_op jit(solution)/shard_map/ppermute | solution.py:294
  8.0 16.1 %collective-permute-start.5 = (bf16[64,2048]{1,0:T(8,128)(2,1)S(1)}, bf16[64,2048]{1,0:T(8,128)(2,1)S(1)}, u32[]{:S(2)}, u32[]{:S(2)}) collective-permute-start(bf16[64,2048]{1,0:T(8,128)(2,1)S(1)} %add_convert_fusion), channel_id=1, source_target_pairs={{0,4},{2,6},{4,0},{6,2},{1,5},{3,7},{5,1},{7,3},{8,12},{10,14},{12... | collective-permute-start | bytes 786440 | tf_op jit(solution)/shard_map/ppermute | solution.py:294
  8.6 15.6 %collective-permute-start.1 = (bf16[64,2048]{1,0:T(8,128)(2,1)S(1)}, bf16[64,2048]{1,0:T(8,128)(2,1)S(1)}, u32[]{:S(2)}, u32[]{:S(2)}) collective-permute-start(bf16[64,2048]{1,0:T(8,128)(2,1)S(1)} %collective-permute-done.second), channel_id=1, source_target_pairs={{0,8},{16,24},{32,40},{48,56},{64,72},{80,88},{96,104},{112,120},{... | collective-permute-start | bytes 786440 | tf_op jit(solution)/shard_map/ppermute | solution.py:294
  14.0 10.2 %collective-permute-start.3 = (bf16[64,2048]{1,0:T(8,128)(2,1)S(1)}, bf16[64,2048]{1,0:T(8,128)(2,1)S(1)}, u32[]{:S(2)}, u32[]{:S(2)}) collective-permute-start(bf16[64,2048]{1,0:T(8,128)(2,1)S(1)} %collective-permute-done.2.first), channel_id=1, source_target_pairs={{8,16},{24,32},{40,48},{56,64},{72,80},{88,96},{104,112},{120,128}... | collective-permute-start | bytes 786440 | tf_op jit(solution)/shard_map/ppermute | solution.py:294
  14.7 42.4 %slice-start = ((s8[8388608]{0:T(1024)(128)(4,1)}), s8[4194304]{0:T(1024)(128)(4,1)S(1)}, s32[]{:S(2)}) async-start(s8[8388608]{0:T(1024)(128)(4,1)} %bitcast.12), calls=%async_computation.2 | async-start | bytes 8388608
  14.7 42.4 %copy-start.3 = (f32[1,64]{1,0:T(1,128)S(1)}, f32[1,64]{1,0:T(1,128)}, u32[]{:S(2)}) copy-start(f32[1,64]{1,0:T(1,128)} %weights.1) | copy-start | bytes 772
  24.2 32.9 %slice-start.1 = ((s8[8388608]{0:T(1024)(128)(4,1)}), s8[4194304]{0:T(1024)(128)(4,1)S(1)}, s32[]{:S(2)}) async-start(s8[8388608]{0:T(1024)(128)(4,1)} %bitcast.12), calls=%async_computation.3 | async-start | bytes 8388608

commit v4 on v3

v4 whole, which is shorter than its diff:
```python
import functools
import math

import jax
import jax.numpy as jnp
from jax import lax
from jax.experimental import pallas as pl
from jax.experimental.pallas import tpu as pltpu
from jax.sharding import PartitionSpec as P

TILE = 256
LANES = 128
GROUPS = 64
EARLY = 4

step_size = 0.5
merging = 0.5
epsilon = 1e-06

NT = (((1,), (1,)), ((), ()))


def place_of():
    return lax.axis_index("genome")


def window_tiles(source, base, shift, count):
    rows = source.shape[0]
    back = lax.rem(LANES - shift, LANES)
    keep = lax.broadcasted_iota(jnp.int32, (rows, LANES), 1) < LANES - shift
    tiles = []
    turned = pltpu.roll(source[:, pl.ds(base, LANES)], back, 1)
    for at in range(count):
        following = pltpu.roll(source[:, pl.ds(base + (at + 1) * LANES, LANES)], back, 1)
        tiles.append(jnp.where(keep, turned, following).astype(jnp.bfloat16))
        turned = following
    return jnp.concatenate(tiles, axis=1)


def unit_copy(band, held, sems, unit, first):
    here = pl.ds(pl.multiple_of((unit - first) * TILE, TILE), TILE)
    there = pl.ds(pl.multiple_of(unit * TILE, TILE), TILE)
    return pltpu.make_async_copy(band.at[there], held.at[here], sems.at[unit - first])


def own_kernel(starts_in, own, band, product, held, padded, starts, sems, start_sem):
    rows, snps = own.shape
    units = held.shape[0] // TILE
    count = snps // TILE + 1
    depth = min(3, units)
    start_copy = pltpu.make_async_copy(starts_in, starts, start_sem)
    start_copy.start()
    for unit in range(depth):
        unit_copy(band, held, sems, unit, 0).start()
    place = place_of()
    padded[:, :snps] = jnp.zeros((rows, snps), jnp.float32)
    padded[:, snps : 2 * snps] = own[...].astype(jnp.float32)
    padded[:, 2 * snps :] = jnp.zeros((rows, padded.shape[1] - 2 * snps), jnp.float32)
    start_copy.wait()

    def per_unit(unit, carry):
        start = starts[0, unit] + (2 - place) * snps
        first_tile = jnp.clip((2 * snps - start) // TILE, 0, snps // TILE - 1)
        column = pl.multiple_of(first_tile * TILE, TILE)
        begin = start + column - snps
        base = pl.multiple_of((begin // LANES) * LANES, LANES)
        window = window_tiles(padded, base, begin - base, count * TILE // LANES)
        cut = pl.ds(pl.multiple_of(unit * TILE, TILE), TILE)
        unit_copy(band, held, sems, unit, 0).wait()

        @pl.when(unit + depth < units)
        def _():
            unit_copy(band, held, sems, unit + depth, 0).start()

        product[:, cut] = lax.dot_general(
            window, held[cut, pl.ds(column, count * TILE)], NT, preferred_element_type=jnp.float32
        )
        return carry

    lax.fori_loop(0, units, per_unit, 0)


def own_step(starts, own, band, units):
    rows, snps = own.shape
    width = band.shape[1]
    hbm = pl.BlockSpec(memory_space=pltpu.HBM)
    vmem = pl.BlockSpec(memory_space=pltpu.VMEM)
    return pl.pallas_call(
        own_kernel,
        in_specs=[hbm, vmem, hbm],
        out_specs=[vmem, vmem],
        out_shape=[
            jax.ShapeDtypeStruct((rows, units * TILE), jnp.float32),
            jax.ShapeDtypeStruct((units * TILE, width), band.dtype),
        ],
        scratch_shapes=[
            pltpu.VMEM((rows, 3 * snps + TILE + LANES), jnp.float32),
            pltpu.SMEM((1, snps // TILE), jnp.int32),
            pltpu.SemaphoreType.DMA((units,)),
            pltpu.SemaphoreType.DMA,
        ],
        compiler_params=pltpu.CompilerParams(vmem_limit_bytes=10 << 20),
        cost_estimate=pl.CostEstimate(
            flops=2 * rows * units * TILE * (snps + TILE), bytes_accessed=2 * units * TILE * width, transcendentals=0
        ),
        name="own_step",
    )(pltpu.with_memory_space_constraint(starts, pltpu.HBM), own, pltpu.with_memory_space_constraint(band, pltpu.HBM))


def near_kernel(
    starts_in, own, first, second, early, before, band, product, late, extended, starts, sems, start_sem
):
    rows, snps = first.shape
    width = band.shape[1]
    units = snps // TILE
    early_units = early.shape[0] // TILE
    count = units + 1
    start_copy = pltpu.make_async_copy(starts_in, starts, start_sem)
    start_copy.start()
    for unit in range(early_units, units):
        unit_copy(band, late, sems, unit, early_units).start()
    place = place_of()
    first_at = jnp.where(lax.rem(place, 2) == 0, 3 * snps, snps)
    for at in (0, 2, 4):
        extended[:, at * snps : (at + 1) * snps] = jnp.zeros((rows, snps), jnp.float32)
    extended[:, 5 * snps :] = jnp.zeros((rows, LANES), jnp.float32)
    for at, piece in ((first_at, first), (4 * snps - first_at, second)):
        extended[:, pl.ds(pl.multiple_of(at, LANES), snps)] = piece[...].astype(jnp.float32)
    start_copy.wait()

    def early_unit(unit, carry):
        start = starts[0, unit] + (2 - place) * snps
        cut = pl.ds(pl.multiple_of(unit * TILE, TILE), TILE)
        left = (2 * snps - start) // TILE
        skip = jnp.where(
            start > 2 * snps, (3 * snps - start) // TILE, jnp.where(start <= snps, (snps - start) // TILE, 0)
        )
        skip = jnp.clip(skip, 0, count - 2)
        both = (start > snps) & (start <= 2 * snps)
        total = before[:, cut]
        for step in range(count):
            tile = step + jnp.where(both & (step > left), count - 2, skip)
            column = pl.multiple_of(tile * TILE, TILE)
            begin = start + column
            base = pl.multiple_of((begin // LANES) * LANES, LANES)
            window = window_tiles(extended, base, begin - base, TILE // LANES)
            total += lax.dot_general(window, early[cut, pl.ds(column, TILE)], NT, preferred_element_type=jnp.float32)
        product[:, cut] = total
        return carry

    lax.fori_loop(0, early_units, early_unit, 0)
    extended[:, 2 * snps : 3 * snps] = own[...].astype(jnp.float32)

    def late_unit(unit, carry):
        start = starts[0, unit] + (2 - place) * snps
        base = pl.multiple_of((start // LANES) * LANES, LANES)
        window = window_tiles(extended, base, start - base, width // LANES)
        unit_copy(band, late, sems, unit, early_units).wait()
        here = pl.ds(pl.multiple_of((unit - early_units) * TILE, TILE), TILE)
        cut = pl.ds(pl.multiple_of(unit * TILE, TILE), TILE)
        product[:, cut] = lax.dot_general(window, late[here, :], NT, preferred_element_type=jnp.float32)
        return carry

    lax.fori_loop(early_units, units, late_unit, 0)


def near_step(starts, own, first, second, early, before, band):
    rows, snps = first.shape
    width = band.shape[1]
    late_rows = snps - early.shape[0]
    hbm = pl.BlockSpec(memory_space=pltpu.HBM)
    vmem = pl.BlockSpec(memory_space=pltpu.VMEM)
    return pl.pallas_call(
        near_kernel,
        in_specs=[hbm] + [vmem] * 5 + [hbm],
        out_specs=[vmem, vmem],
        out_shape=[
            jax.ShapeDtypeStruct((rows, snps), jnp.float32),
            jax.ShapeDtypeStruct((late_rows, width), band.dtype),
        ],
        scratch_shapes=[
            pltpu.VMEM((rows, 5 * snps + LANES), jnp.float32),
            pltpu.SMEM((1, snps // TILE), jnp.int32),
            pltpu.SemaphoreType.DMA((late_rows // TILE,)),
            pltpu.SemaphoreType.DMA,
        ],
        compiler_params=pltpu.CompilerParams(vmem_limit_bytes=10 << 20),
        cost_estimate=pl.CostEstimate(
            flops=2 * rows * snps * width, bytes_accessed=2 * late_rows * width + 8 * rows * snps, transcendentals=0
        ),
        name="near_step",
    )(
        pltpu.with_memory_space_constraint(starts, pltpu.HBM), own, first, second, early, before,
        pltpu.with_memory_space_constraint(band, pltpu.HBM),
    )


def far_kernel(
    ancestries, starts_in, first, second, early, late, product, coef, targets, core_copy, pair_copy, ids,
    proposal, sums, far, square_acc, count_acc, starts, start_sem,
):
    rows, snps = coef.shape
    units = snps // TILE
    reach = 2 * TILE
    place = place_of()
    high_at = snps + 4 * TILE
    first_at = jnp.where(lax.rem(place, 2) == 0, high_at, 0)
    start_copy = pltpu.make_async_copy(starts_in, starts, start_sem)
    start_copy.start()
    far[:, snps:high_at] = jnp.zeros((rows, high_at - snps), jnp.float32)
    far[:, high_at + snps :] = jnp.zeros((rows, LANES), jnp.float32)
    for at, piece in ((first_at, first), (high_at - first_at, second)):
        far[:, pl.ds(pl.multiple_of(at, LANES), piece.shape[1])] = piece[...].astype(jnp.float32)
    square_acc[...] = jnp.zeros_like(square_acc)
    count_acc[...] = jnp.zeros_like(count_acc)
    start_copy.wait()
    group = lax.broadcasted_iota(jnp.int32, (GROUPS, LANES), 0)

    def per_unit(held, first_unit, unit, carry):
        cut = pl.ds(pl.multiple_of(unit * TILE, TILE), TILE)
        here = pl.ds(pl.multiple_of((unit - first_unit) * TILE, TILE), TILE)
        start = starts[0, unit] + (2 - place) * snps
        tiles = held.shape[1] // TILE
        low_count = (jnp.maximum(snps - start, 0) + reach - 1) // reach
        high_count = (jnp.maximum(start - 2 * snps, 0) + reach - 1) // reach
        from_tile = jnp.where(high_count > 0, tiles - 2 * high_count, 0)
        moved = start + jnp.where(high_count > 0, high_at - 4 * snps, 0)

        def per_tile(step, total):
            column = pl.multiple_of((from_tile + 2 * step) * TILE, TILE)
            begin = moved + column
            base = pl.multiple_of((begin // LANES) * LANES, LANES)
            window = window_tiles(far, base, begin - base, reach // LANES)
            return total + lax.dot_general(
                window, held[here, pl.ds(column, reach)], NT, preferred_element_type=jnp.float32
            )

        bands = lax.fori_loop(0, low_count + high_count, per_tile, product[:, cut])
        current = coef[:, cut]
        total = current + core_copy[:, cut].astype(jnp.float32) + pair_copy[:, cut].astype(jnp.float32)
        gradient = current + bands - targets[:, cut] + merging * (current - total * (1.0 / ancestries))
        value = current - step_size * gradient
        proposal[:, cut] = value
        part = jnp.sum(value * value, axis=0, keepdims=True)
        ids_here = ids[:, cut]
        squares = square_acc[...]
        counts = count_acc[...]
        for at in range(TILE // LANES):
            here = ids_here[:, at * LANES : (at + 1) * LANES] == group
            squares += jnp.where(here, part[:, at * LANES : (at + 1) * LANES], 0.0)
            counts += jnp.where(here, 1.0, 0.0)
        square_acc[...] = squares
        count_acc[...] = counts
        return carry

    early_units = early.shape[0] // TILE
    lax.fori_loop(0, early_units, functools.partial(per_unit, early, 0), 0)
    lax.fori_loop(early_units, units, functools.partial(per_unit, late, early_units), 0)
    lane = lax.broadcasted_iota(jnp.int32, (GROUPS, LANES), 1)
    square_col = jnp.sum(square_acc[...], axis=1, keepdims=True)
    count_col = jnp.sum(count_acc[...], axis=1, keepdims=True)
    both = jnp.where(lane == group, square_col, 0.0) + jnp.where(lane == group + GROUPS, count_col * rows, 0.0)
    sums[...] = jnp.broadcast_to(jnp.sum(both, axis=0, keepdims=True), sums.shape)


def far_step(starts, first, second, early, late, product, coef, targets, core_copy, pair_copy, ids, peers, ancestries):
    rows, snps = coef.shape
    hbm = pl.BlockSpec(memory_space=pltpu.HBM)
    vmem = pl.BlockSpec(memory_space=pltpu.VMEM)
    return pl.pallas_call(
        functools.partial(far_kernel, ancestries),
        in_specs=[hbm] + [vmem] * 10,
        out_specs=[vmem, vmem],
        out_shape=[
            jax.ShapeDtypeStruct((rows, snps), jnp.float32),
            jax.ShapeDtypeStruct((peers, LANES), jnp.float32),
        ],
        scratch_shapes=[
            pltpu.VMEM((rows, 2 * snps + 4 * TILE + LANES), jnp.float32),
            pltpu.VMEM((GROUPS, LANES), jnp.float32),
            pltpu.VMEM((GROUPS, LANES), jnp.float32),
            pltpu.SMEM((1, snps // TILE), jnp.int32),
            pltpu.SemaphoreType.DMA,
        ],
        compiler_params=pltpu.CompilerParams(vmem_limit_bytes=10 << 20),
        cost_estimate=pl.CostEstimate(
            flops=2 * rows * snps * 1024, bytes_accessed=20 * rows * snps, transcendentals=0
        ),
        name="far_step",
    )(
        pltpu.with_memory_space_constraint(starts, pltpu.HBM), first, second, early, late, product, coef, targets, core_copy, pair_copy, ids,
    )


def score_kernel(scale, sums, weights, ids, proposal, dosage, updated_out, partial, low, updated, out_sem):
    rows, snps = proposal.shape
    block = TILE
    total = jnp.sum(sums[...], axis=0, keepdims=True)
    spread = jnp.broadcast_to(total, (GROUPS, LANES))
    group = lax.broadcasted_iota(jnp.int32, (GROUPS, LANES), 0)
    place = lax.broadcasted_iota(jnp.int32, (GROUPS, LANES), 1)
    squares = jnp.sum(jnp.where(place == group, spread, 0.0), axis=1, keepdims=True)
    counts = jnp.sum(jnp.where(place == group + GROUPS, spread, 0.0), axis=1, keepdims=True)
    weight_row = jnp.broadcast_to(weights[...], (GROUPS, GROUPS))
    here = lax.broadcasted_iota(jnp.int32, (GROUPS, GROUPS), 0) == lax.broadcasted_iota(
        jnp.int32, (GROUPS, GROUPS), 1
    )
    weight = jnp.sum(jnp.where(here, weight_row, 0.0), axis=1, keepdims=True)
    threshold = step_size * weight * jnp.sqrt(counts)
    factor = jnp.maximum(0.0, 1.0 - threshold / jnp.sqrt(squares + epsilon))
    factor = jnp.broadcast_to(factor, (GROUPS, LANES))
    for at in range(snps // LANES):
        cut = slice(at * LANES, (at + 1) * LANES)
        chosen = jnp.sum(jnp.where(ids[:, cut] == group, factor, 0.0), axis=0, keepdims=True)
        value = proposal[:, cut] * chosen
        updated[:, cut] = value
        low[:, cut] = value.astype(jnp.bfloat16)
    write_out = pltpu.make_async_copy(updated, updated_out, out_sem)
    write_out.start()
    half = rows // 2
    left = lax.broadcasted_iota(jnp.int32, (half, LANES), 1) < LANES // 2

    def per_block(step, carry):
        people = pl.ds(pl.multiple_of(step * block, block), block)
        product = lax.dot_general(low[...], dosage[people, :], NT, preferred_element_type=jnp.float32) * scale
        for at in range(block // LANES):
            cut = product[:, at * LANES : (at + 1) * LANES]
            first, second = cut[:half], cut[half:]
            index = step * (2 * block // LANES) + 2 * at
            partial[index] = jnp.where(left, first, pltpu.roll(second, LANES // 2, 1)).astype(partial.dtype)
            partial[index + 1] = jnp.where(left, pltpu.roll(first, LANES // 2, 1), second).astype(partial.dtype)
        return carry

    lax.fori_loop(0, dosage.shape[0] // block, per_block, 0)
    write_out.wait()


def score_step(sums, weights, ids, proposal, dosage, genome_count):
    rows, snps = proposal.shape
    persons = dosage.shape[0]
    vmem = pl.BlockSpec(memory_space=pltpu.VMEM)
    return pl.pallas_call(
        functools.partial(score_kernel, 1.0 / math.sqrt(snps * genome_count)),
        in_specs=[vmem] * 5,
        out_specs=[pl.BlockSpec(memory_space=pltpu.HBM), vmem],
        out_shape=[
            jax.ShapeDtypeStruct((rows, snps), jnp.float32),
            jax.ShapeDtypeStruct((genome_count, rows // 2, LANES), jnp.bfloat16),
        ],
        scratch_shapes=[
            pltpu.VMEM((rows, snps), jnp.bfloat16),
            pltpu.VMEM((rows, snps), jnp.float32),
            pltpu.SemaphoreType.DMA,
        ],
        compiler_params=pltpu.CompilerParams(vmem_limit_bytes=8 << 20),
        cost_estimate=pl.CostEstimate(
            flops=2 * rows * snps * persons, bytes_accessed=2 * snps * persons + 8 * rows * snps, transcendentals=0
        ),
        name="score_step",
    )(sums, weights, ids, proposal, dosage)


def total_kernel(arrived, scores):
    total = jnp.sum(arrived[...].astype(jnp.float32), axis=0)
    half = LANES // 2
    rows = total.shape[0]
    scores[:rows] = total[:, :half]
    scores[rows:] = pltpu.roll(total, half, 1)[:, :half]


def total_step(arrived):
    rows = 2 * arrived.shape[1]
    return pl.pallas_call(
        total_kernel,
        in_specs=[pl.BlockSpec(memory_space=pltpu.VMEM)],
        out_specs=pl.BlockSpec(memory_space=pltpu.VMEM),
        out_shape=jax.ShapeDtypeStruct((rows, LANES // 2), jnp.float32),
        name="total_step",
    )(arrived)


def swapped(block, axis, distance, lower):
    count = lax.axis_size(axis)
    pairs = [(i, i + distance) for i in range(count - distance) if lower(i)]
    return lax.ppermute(block, axis, pairs + [(j, i) for i, j in pairs])


def per_device(coefficients, sumstats, linkage, band_start, group_ids, group_weight, dosage):
    current = coefficients[0]
    targets = sumstats[0]
    band = linkage[0]
    genome_count = lax.axis_size("genome")
    anc_count = lax.axis_size("anc")
    low_copy = current.astype(jnp.bfloat16)
    near_even = swapped(low_copy, "genome", 1, lambda i: i % 2 == 0)
    near_odd = swapped(low_copy, "genome", 1, lambda i: i % 2 == 1)
    core_copy = swapped(low_copy, "anc", 1, lambda i: i % 2 == 0)
    pair_sum = (current + core_copy.astype(jnp.float32)).astype(jnp.bfloat16)
    pair_sum, own_copy = lax.optimization_barrier((pair_sum, low_copy))
    pair_copy = swapped(pair_sum, "anc", 2, lambda i: i < 2)
    own_product, early = own_step(band_start, own_copy, band, EARLY)
    near_even, near_odd, own_product = lax.optimization_barrier((near_even, near_odd, own_product))
    far_even = swapped(near_odd, "genome", 1, lambda i: i % 2 == 0)
    far_odd = swapped(near_even, "genome", 1, lambda i: i % 2 == 1)
    product, late = near_step(band_start, low_copy, near_even, near_odd, early, own_product, band)
    peers = genome_count * lax.axis_size("trait")
    proposal, sums = far_step(
        band_start, far_even, far_odd, early, late, product, current, targets, core_copy, pair_copy,
        group_ids, peers, anc_count,
    )
    arrived = lax.all_to_all(
        sums.reshape(peers, 1, LANES), ("genome", "trait"), split_axis=0, concat_axis=0, tiled=True
    ).reshape(peers, LANES)
    updated, partial = score_step(arrived, group_weight, group_ids, proposal, dosage[0], genome_count)
    received = lax.all_to_all(partial, "genome", split_axis=0, concat_axis=0, tiled=True)
    scores = total_step(received)
    return (updated[None], scores[None])


def solution(mesh):
    in_specs = (
        P("anc", "trait", "genome"),
        P("anc", "trait", "genome"),
        P("anc", "genome", None),
        P("anc", "genome"),
        P("anc", "genome"),
        P("anc", None),
        P("anc", None, "genome"),
    )
    out_specs = (P("anc", "trait", "genome"), P("anc", "trait", "genome"))
    return jax.shard_map(
        per_device, mesh=mesh, in_specs=in_specs, out_specs=out_specs, check_vma=False
    )
```

time: 80 us -> 78.7 us (0.984)
  starting transfers between devices: 11.7 us -> 8.9 us
  Pallas kernels: 18.3 us -> 19.6 us
  waiting for transfers between devices: 0.02 us -> 0.94 us
    ppermute x6, starting transfers between devices: 11.7 us -> 8.9 us  [swapped(): return lax.ppermute(block, axis, pairs + [(j, i) for i, j in pairs])]
    pallas_call x2 -> x3, Pallas kernels: 11.1 us -> 13.1 us  [the longest x1 7.05 us: near_step(): pl.pallas_call(near_kernel, in_specs=[hbm] + [vmem] * 5 + [hbm], out_spec...]
    ppermute x6, waiting for transfers between devices: 0.02 us -> 0.94 us  [swapped(): return lax.ppermute(block, axis, pairs + [(j, i) for i, j in pairs])]
  transfers between devices with their start and end apart: 6 -> 6, of which waited for: 0 -> 1; matrix products, arithmetic and copies ran while one was open for 1% -> 1% of each run, Pallas kernels for 12% -> 15%
where the time goes in v4:
time: 78.7 us; the launch traced here: 78 us
  blocking collectives  45.6 us (58%)
  Pallas kernels  19.6 us (25%)
  starting transfers between devices  8.9 us (11%)
  other arithmetic  2.18 us (3%)
  waiting for transfers between devices  0.94 us (1%)
    all_to_all x1, blocking collectives, per_device(): lax.all_to_all(sums.reshape(peers, 1, LANES), ('genome', 'trait'), split_...  30.2 us
    all_to_all x1, blocking collectives, per_device(): lax.all_to_all(partial, 'genome', split_axis=0, concat_axis=0, tiled=True)  15.4 us
    ppermute x6, starting transfers between devices, swapped(): return lax.ppermute(block, axis, pairs + [(j, i) for i, j in pairs])  8.9 us
    pallas_call x1, Pallas kernels, near_step(): pl.pallas_call(near_kernel, in_specs=[hbm] + [vmem] * 5 + [hbm], out_spec...  7.05 us
    pallas_call x1, Pallas kernels, score_step(): pl.pallas_call(functools.partial(score_kernel, 1.0 / math.sqrt(snps * gen...  4.49 us
    pallas_call x1, Pallas kernels, own_step(): pl.pallas_call(own_kernel, in_specs=[hbm, vmem, hbm], out_specs=[vmem, vm...  4.4 us
    pallas_call x1, Pallas kernels, far_step(): pl.pallas_call(functools.partial(far_kernel, ancestries), in_specs=[hbm]...  1.95 us
    pallas_call x1, Pallas kernels, total_step(): pl.pallas_call(total_kernel, in_specs=[pl.BlockSpec(memory_space=pltpu.VM...  1.68 us
  transfers between devices with their start and end apart: 6, of which 1 were waited for; matrix products, arithmetic and copies ran while one was open for 1% of the time, Pallas kernels for 15%

profile of v4, /device:TPU:8, one launch (start us, length us, event | category | flops | bytes accessed | tf_op | source)
XLA Modules:
  0.0 78.0 jit_solution(16590387430650939712)
XLA Ops:
  0.6 1.1 %bitcast_convert_fusion.own = bf16[64,2048]{1,0:T(8,128)(2,1)S(1)} fusion(f32[1,64,2048]{2,1,0:T(8,128)} %param.7), kind=kLoop, calls=%fused_computation.1 | loop fusion | flops 131072 | bytes 786432 | tf_op jit(solution)/shard_map/convert_element_type | solution.py:394
  1.7 0.1 collective-permute-start.2
  1.8 1.6 %collective-permute-start = (bf16[64,2048]{1,0:T(8,128)(2,1)S(1)}, bf16[64,2048]{1,0:T(8,128)(2,1)S(1)}, u32[]{:S(2)}, u32[]{:S(2)}) collective-permute-start(bf16[64,2048]{1,0:T(8,128)(2,1)S(1)} %bitcast_convert_fusion.own), channel_id=1, source_target_pairs={{0,8},{16,24},{32,40},{48,56},{64,72},{80,88},{96,104},{112,120},{... | collective-permute-start | bytes 786440 | tf_op jit(solution)/shard_map/ppermute | solution.py:385
  3.4 0.7 collective-permute-start.1
  4.1 0.0 collective-permute-done.2.core_copy
  4.1 1.1 %add_convert_fusion = bf16[64,2048]{1,0:T(8,128)(2,1)S(1)} fusion(bf16[64,2048]{1,0:T(8,128)(2,1)S(1)} %collective-permute-done.2.core_copy, f32[1,64,2048]{2,1,0:T(8,128)} %param.7), kind=kLoop, calls=%fused_computation | loop fusion | flops 393216 | bytes 1048576 | tf_op jit(solution)/shard_map/convert_element_type | solution.py:398
  5.2 0.0 slice-start
  5.2 4.4 %own_step.1 = (f32[64,1024]{1,0:T(8,128)S(1)}, bf16[1024,4096]{1,0:T(8,128)(2,1)S(1)}) custom-call(s32[1,8]{1,0:T(1,128)} %starts_in.5, bf16[64,2048]{1,0:T(8,128)(2,1)S(1)} %bitcast_convert_fusion.own, bf16[2048,4096]{1,0:T(8,128)(2,1)} %bitcast.19), custom_call_target="tpu_custom_call" | custom-call | flops 301989888 | bytes 8388608 | tf_op jit(solution)/shard_map/own_step/pallas_call | solution.py:88
  9.6 0.9 %collective-permute-done.first = bf16[64,2048]{1,0:T(8,128)(2,1)S(1)} collective-permute-done((bf16[64,2048]{1,0:T(8,128)(2,1)S(1)}, bf16[64,2048]{1,0:T(8,128)(2,1)S(1)}, u32[]{:S(2)}, u32[]{:S(2)}) %collective-permute-start) | collective-permute-done | bytes 262176 | tf_op jit(solution)/shard_map/ppermute | solution.py:385
  10.5 0.0 collective-permute-done.1.second
  10.5 4.0 %collective-permute-start.3 = (bf16[64,2048]{1,0:T(8,128)(2,1)S(1)}, bf16[64,2048]{1,0:T(8,128)(2,1)S(1)}, u32[]{:S(2)}, u32[]{:S(2)}) collective-permute-start(bf16[64,2048]{1,0:T(8,128)(2,1)S(1)} %collective-permute-done.1.second), channel_id=1, source_target_pairs={{0,8},{16,24},{32,40},{48,56},{64,72},{80,88},{96,104},{112,120},{... | collective-permute-start | bytes 786440 | tf_op jit(solution)/shard_map/ppermute | solution.py:385
  14.6 0.7 collective-permute-start.4
  15.3 1.9 %collective-permute-start.5 = (bf16[64,2048]{1,0:T(8,128)(2,1)S(1)}, bf16[64,2048]{1,0:T(8,128)(2,1)S(1)}, u32[]{:S(2)}, u32[]{:S(2)}) collective-permute-start(bf16[64,2048]{1,0:T(8,128)(2,1)S(1)} %add_convert_fusion), channel_id=1, source_target_pairs={{0,4},{2,6},{4,0},{6,2},{1,5},{3,7},{5,1},{7,3},{8,12},{10,14},{12... | collective-permute-start | bytes 786440 | tf_op jit(solution)/shard_map/ppermute | solution.py:385
  17.1 7.0 %near_step.1 = (f32[64,2048]{1,0:T(8,128)S(1)}, bf16[1024,4096]{1,0:T(8,128)(2,1)S(1)}) custom-call(s32[1,8]{1,0:T(1,128)} %starts_in.5, bf16[64,2048]{1,0:T(8,128)(2,1)S(1)} %bitcast_convert_fusion.own, bf16[64,2048]{1,0:T(8,128)(2,1)S(1)} %collective-permute-done.first, bf16[64,2048]{1,0:T(8,128)(2,1)S(1)} %collective-permute-done.1.second, ...), custom_call_target="tpu_custom_call" | custom-call | flops 1073741824 | bytes 9437184 | tf_op jit(solution)/shard_map/near_step/pallas_call | solution.py:173
  24.2 0.0 collective-permute-done.3.first
  24.2 0.0 collective-permute-done.4.second
  24.2 0.0 collective-permute-done.5.pair_copy
  24.2 0.0 copy-done
  24.2 0.0 copy-start.3
  24.2 1.9 %far_step.1 = (f32[64,2048]{1,0:T(8,128)S(1)}, f32[64,128]{1,0:T(8,128)S(1)}) custom-call(s32[1,8]{1,0:T(1,128)} %starts_in.5, bf16[64,2048]{1,0:T(8,128)(2,1)S(1)} %collective-permute-done.3.first, bf16[64,2048]{1,0:T(8,128)(2,1)S(1)} %collective-permute-done.4.second, bf16[1024,4096]{1,0:T(8,128)(2,1)S(1)} %get-tuple-element.19.early, ...), custom_call_target="tpu_custom_call" | custom-call | flops 268435456 | bytes 2621440 | tf_op jit(solution)/shard_map/far_step/pallas_call | solution.py:270
  26.2 30.2 %all_to_all.10 = f32[64,1,128]{2,1,0:T(1,128)S(1)} all-to-all(f32[64,1,128]{2,1,0:T(1,128)S(1)} %bitcast.18), channel_id=1, replica_groups=mesh['genome'=32,'anc'=4,'trait'=2] {'genome','trait'}, dimensions={0} | all-to-all | bytes 65536 | tf_op jit(solution)/shard_map/all_to_all | solution.py:411
  56.4 4.5 %score_step.1 = (f32[64,2048]{1,0:T(8,128)}, bf16[32,32,128]{2,1,0:T(8,128)(2,1)S(1)}) custom-call(f32[64,128]{1,0:T(8,128)S(1)} %bitcast.17, f32[1,64]{1,0:T(1,128)S(1)} %copy-done.3, s32[1,2048]{1,0:T(1,128)S(1)} %copy-done.2, f32[64,2048]{1,0:T(8,128)S(1)} %get-tuple-element.25.proposal, bf16[2048,2048]{1,0:T(8,128)(2,1)S(1)} %bitcast.14), custom_call_target="tpu_custom_call" | custom-call | flops 536870912 | bytes 9437184 | tf_op jit(solution)/shard_map/score_step/pallas_call | solution.py:342
  60.9 15.4 %all_to_all.11.arrived = bf16[32,32,128]{2,1,0:T(8,128)(2,1)} all-to-all(bf16[32,32,128]{2,1,0:T(8,128)(2,1)S(1)} %get-tuple-element.27), channel_id=1, replica_groups=mesh['genome'=32,'anc'=4,'trait'=2] {'genome'}, dimensions={0} | all-to-all | bytes 524288 | tf_op jit(solution)/shard_map/all_to_all | solution.py:415
  76.3 1.7 %total_step.1 = f32[64,64]{1,0:T(8,128)} custom-call(bf16[32,32,128]{2,1,0:T(8,128)(2,1)} %all_to_all.11.arrived), custom_call_target="tpu_custom_call" | custom-call | tf_op jit(solution)/shard_map/total_step/pallas_call | solution.py:373
  (10 shorter events, 0.0 us)
Async XLA Ops:
  1.7 2.4 %collective-permute-start.2 = (bf16[64,2048]{1,0:T(8,128)(2,1)S(1)}, bf16[64,2048]{1,0:T(8,128)(2,1)S(1)}, u32[]{:S(2)}, u32[]{:S(2)}) collective-permute-start(bf16[64,2048]{1,0:T(8,128)(2,1)S(1)} %bitcast_convert_fusion.own), channel_id=1, source_target_pairs={{0,2},{4,6},{2,0},{6,4},{1,3},{5,7},{3,1},{7,5},{8,10},{12,14},{10... | collective-permute-start | bytes 786440 | tf_op jit(solution)/shard_map/ppermute | solution.py:385
  1.8 8.7 %collective-permute-start = (bf16[64,2048]{1,0:T(8,128)(2,1)S(1)}, bf16[64,2048]{1,0:T(8,128)(2,1)S(1)}, u32[]{:S(2)}, u32[]{:S(2)}) collective-permute-start(bf16[64,2048]{1,0:T(8,128)(2,1)S(1)} %bitcast_convert_fusion.own), channel_id=1, source_target_pairs={{0,8},{16,24},{32,40},{48,56},{64,72},{80,88},{96,104},{112,120},{... | collective-permute-start | bytes 786440 | tf_op jit(solution)/shard_map/ppermute | solution.py:385
  3.4 7.2 %collective-permute-start.1 = (bf16[64,2048]{1,0:T(8,128)(2,1)S(1)}, bf16[64,2048]{1,0:T(8,128)(2,1)S(1)}, u32[]{:S(2)}, u32[]{:S(2)}) collective-permute-start(bf16[64,2048]{1,0:T(8,128)(2,1)S(1)} %bitcast_convert_fusion.own), channel_id=1, source_target_pairs={{8,16},{24,32},{40,48},{56,64},{72,80},{88,96},{104,112},{120,128}... | collective-permute-start | bytes 786440 | tf_op jit(solution)/shard_map/ppermute | solution.py:385
  5.2 51.2 %slice-start = ((s8[8388608]{0:T(1024)(128)(4,1)}), s8[4194304]{0:T(1024)(128)(4,1)S(1)}, s32[]{:S(2)}) async-start(s8[8388608]{0:T(1024)(128)(4,1)} %bitcast.12), calls=%async_computation.2 | async-start | bytes 8388608
  10.5 13.6 %collective-permute-start.3 = (bf16[64,2048]{1,0:T(8,128)(2,1)S(1)}, bf16[64,2048]{1,0:T(8,128)(2,1)S(1)}, u32[]{:S(2)}, u32[]{:S(2)}) collective-permute-start(bf16[64,2048]{1,0:T(8,128)(2,1)S(1)} %collective-permute-done.1.second), channel_id=1, source_target_pairs={{0,8},{16,24},{32,40},{48,56},{64,72},{80,88},{96,104},{112,120},{... | collective-permute-start | bytes 786440 | tf_op jit(solution)/shard_map/ppermute | solution.py:385
  14.6 9.6 %collective-permute-start.4 = (bf16[64,2048]{1,0:T(8,128)(2,1)S(1)}, bf16[64,2048]{1,0:T(8,128)(2,1)S(1)}, u32[]{:S(2)}, u32[]{:S(2)}) collective-permute-start(bf16[64,2048]{1,0:T(8,128)(2,1)S(1)} %collective-permute-done.first), channel_id=1, source_target_pairs={{8,16},{24,32},{40,48},{56,64},{72,80},{88,96},{104,112},{120,128}... | collective-permute-start | bytes 786440 | tf_op jit(solution)/shard_map/ppermute | solution.py:385
  15.3 8.9 %collective-permute-start.5 = (bf16[64,2048]{1,0:T(8,128)(2,1)S(1)}, bf16[64,2048]{1,0:T(8,128)(2,1)S(1)}, u32[]{:S(2)}, u32[]{:S(2)}) collective-permute-start(bf16[64,2048]{1,0:T(8,128)(2,1)S(1)} %add_convert_fusion), channel_id=1, source_target_pairs={{0,4},{2,6},{4,0},{6,2},{1,5},{3,7},{5,1},{7,3},{8,12},{10,14},{12... | collective-permute-start | bytes 786440 | tf_op jit(solution)/shard_map/ppermute | solution.py:385
  17.1 7.1 %copy-start = (f32[1,64,2048]{2,1,0:T(8,128)S(1)}, f32[1,64,2048]{2,1,0:T(8,128)}, u32[]{:S(2)}) copy-start(f32[1,64,2048]{2,1,0:T(8,128)} %param.7) | copy-start | bytes 1572868
  17.1 7.1 %copy-start.1 = (f32[1,64,2048]{2,1,0:T(8,128)S(1)}, f32[1,64,2048]{2,1,0:T(8,128)}, u32[]{:S(2)}) copy-start(f32[1,64,2048]{2,1,0:T(8,128)} %param.8) | copy-start | bytes 1572868
  17.1 7.1 %copy-start.2 = (s32[1,2048]{1,0:T(1,128)S(1)}, s32[1,2048]{1,0:T(1,128)}, u32[]{:S(2)}) copy-start(s32[1,2048]{1,0:T(1,128)} %ids.3) | copy-start | bytes 24580
  17.1 39.3 %slice-start.1 = ((s8[8388608]{0:T(1024)(128)(4,1)}), s8[4194304]{0:T(1024)(128)(4,1)S(1)}, s32[]{:S(2)}) async-start(s8[8388608]{0:T(1024)(128)(4,1)} %bitcast.12), calls=%async_computation.3 | async-start | bytes 8388608
  24.2 32.2 %copy-start.3 = (f32[1,64]{1,0:T(1,128)S(1)}, f32[1,64]{1,0:T(1,128)}, u32[]{:S(2)}) copy-start(f32[1,64]{1,0:T(1,128)} %weights.1) | copy-start | bytes 772

commit v5 on v4

--- a/solution.py
+++ b/solution.py
@@ -11,7 +11,7 @@
 TILE = 256
 LANES = 128
 GROUPS = 64
-EARLY = 4
+EARLY = 7
 
 step_size = 0.5
 merging = 0.5
@@ -197,13 +197,13 @@
 
 def far_kernel(
     ancestries, starts_in, first, second, early, late, product, coef, targets, core_copy, pair_copy, ids,
-    proposal, sums, far, square_acc, count_acc, starts, start_sem,
+    proposal, sums, far, square_acc, count_acc, bands_ref, starts, start_sem,
 ):
     rows, snps = coef.shape
     units = snps // TILE
-    reach = 2 * TILE
+    widths = (0, 2, 4, 8)
     place = place_of()
-    high_at = snps + 4 * TILE
+    high_at = 2 * snps + TILE
     first_at = jnp.where(lax.rem(place, 2) == 0, high_at, 0)
     start_copy = pltpu.make_async_copy(starts_in, starts, start_sem)
     start_copy.start()
@@ -221,21 +221,27 @@
         here = pl.ds(pl.multiple_of((unit - first_unit) * TILE, TILE), TILE)
         start = starts[0, unit] + (2 - place) * snps
         tiles = held.shape[1] // TILE
-        low_count = (jnp.maximum(snps - start, 0) + reach - 1) // reach
-        high_count = (jnp.maximum(start - 2 * snps, 0) + reach - 1) // reach
-        from_tile = jnp.where(high_count > 0, tiles - 2 * high_count, 0)
-        moved = start + jnp.where(high_count > 0, high_at - 4 * snps, 0)
-
-        def per_tile(step, total):
-            column = pl.multiple_of((from_tile + 2 * step) * TILE, TILE)
-            begin = moved + column
-            base = pl.multiple_of((begin // LANES) * LANES, LANES)
-            window = window_tiles(far, base, begin - base, reach // LANES)
-            return total + lax.dot_general(
-                window, held[here, pl.ds(column, reach)], NT, preferred_element_type=jnp.float32
-            )
-
-        bands = lax.fori_loop(0, low_count + high_count, per_tile, product[:, cut])
+        low_count = (jnp.maximum(snps - start, 0) + TILE - 1) // TILE
+        high_count = (jnp.maximum(start - 2 * snps, 0) + TILE - 1) // TILE
+        above = high_count > 0
+        needed = low_count + high_count
+        choice = sum((needed > width).astype(jnp.int32) for width in widths[:-1])
+        bands_ref[...] = product[:, cut]
+        for option, width in enumerate(widths):
+            if width == 0:
+                continue
+
+            @pl.when(choice == option)
+            def _():
+                column = pl.multiple_of(jnp.where(above, tiles - width, 0) * TILE, TILE)
+                begin = start + column + jnp.where(above, high_at - 4 * snps, 0)
+                base = pl.multiple_of((begin // LANES) * LANES, LANES)
+                window = window_tiles(far, base, begin - base, width * TILE // LANES)
+                bands_ref[...] += lax.dot_general(
+                    window, held[here, pl.ds(column, width * TILE)], NT, preferred_element_type=jnp.float32
+                )
+
+        bands = bands_ref[...]
         current = coef[:, cut]
         total = current + core_copy[:, cut].astype(jnp.float32) + pair_copy[:, cut].astype(jnp.float32)
         gradient = current + bands - targets[:, cut] + merging * (current - total * (1.0 / ancestries))
@@ -276,9 +282,10 @@
             jax.ShapeDtypeStruct((peers, LANES), jnp.float32),
         ],
         scratch_shapes=[
-            pltpu.VMEM((rows, 2 * snps + 4 * TILE + LANES), jnp.float32),
+            pltpu.VMEM((rows, 3 * snps + TILE + LANES), jnp.float32),
             pltpu.VMEM((GROUPS, LANES), jnp.float32),
             pltpu.VMEM((GROUPS, LANES), jnp.float32),
+            pltpu.VMEM((rows, TILE), jnp.float32),
             pltpu.SMEM((1, snps // TILE), jnp.int32),
             pltpu.SemaphoreType.DMA,
         ],

time: 78.7 us -> 77.9 us (0.990)
  Pallas kernels: 19.6 us -> 20.7 us
  starting transfers between devices: 8.9 us -> 7.97 us
    pallas_call x1, Pallas kernels: 4.4 us -> 6.27 us  [own_step(): pl.pallas_call(own_kernel, in_specs=[hbm, vmem, hbm], out_specs=[vmem, vm...]
    pallas_call x1, Pallas kernels: 7.05 us -> 5.77 us  [near_step(): pl.pallas_call(near_kernel, in_specs=[hbm] + [vmem] * 5 + [hbm], out_spec...]
    ppermute x6, starting transfers between devices: 8.9 us -> 7.97 us  [swapped(): return lax.ppermute(block, axis, pairs + [(j, i) for i, j in pairs])]
    all_to_all x1, blocking collectives: 30.2 us -> 29.4 us  [per_device(): lax.all_to_all(sums.reshape(peers, 1, LANES), ('genome', 'trait'), split_...]
  transfers between devices with their start and end apart: 6 -> 6, of which waited for: 1 -> 1; matrix products, arithmetic and copies ran while one was open for 1% -> 1% of each run, Pallas kernels for 15% -> 16%
where the time goes in v5:
time: 77.9 us; the launch traced here: 77.6 us
  blocking collectives  44.9 us (58%)
  Pallas kernels  20.7 us (27%)
  starting transfers between devices  7.97 us (10%)
  other arithmetic  2.16 us (3%)
  waiting for transfers between devices  1.11 us (1%)
  between operations  0.78 us (1%)
    all_to_all x1, blocking collectives, per_device(): lax.all_to_all(sums.reshape(peers, 1, LANES), ('genome', 'trait'), split_...  29.4 us
    all_to_all x1, blocking collectives, per_device(): lax.all_to_all(partial, 'genome', split_axis=0, concat_axis=0, tiled=True)  15.5 us
    ppermute x6, starting transfers between devices, swapped(): return lax.ppermute(block, axis, pairs + [(j, i) for i, j in pairs])  7.97 us
    pallas_call x1, Pallas kernels, own_step(): pl.pallas_call(own_kernel, in_specs=[hbm, vmem, hbm], out_specs=[vmem, vm...  6.27 us
    pallas_call x1, Pallas kernels, near_step(): pl.pallas_call(near_kernel, in_specs=[hbm] + [vmem] * 5 + [hbm], out_spec...  5.77 us
    pallas_call x1, Pallas kernels, score_step(): pl.pallas_call(functools.partial(score_kernel, 1.0 / math.sqrt(snps * gen...  4.49 us
    pallas_call x1, Pallas kernels, far_step(): pl.pallas_call(functools.partial(far_kernel, ancestries), in_specs=[hbm]...  2.51 us
    pallas_call x1, Pallas kernels, total_step(): pl.pallas_call(total_kernel, in_specs=[pl.BlockSpec(memory_space=pltpu.VM...  1.68 us
  transfers between devices with their start and end apart: 6, of which 1 were waited for; matrix products, arithmetic and copies ran while one was open for 1% of the time, Pallas kernels for 16%

profile of v5, /device:TPU:8, one launch (start us, length us, event | category | flops | bytes accessed | tf_op | source)
XLA Modules:
  0.0 77.6 jit_solution(16833625179995262752)
XLA Ops:
  0.6 1.1 %bitcast_convert_fusion.own = bf16[64,2048]{1,0:T(8,128)(2,1)S(1)} fusion(f32[1,64,2048]{2,1,0:T(8,128)} %param.7), kind=kLoop, calls=%fused_computation.1 | loop fusion | flops 131072 | bytes 786432 | tf_op jit(solution)/shard_map/convert_element_type | solution.py:401
  1.7 0.1 collective-permute-start.2
  1.8 1.6 %collective-permute-start = (bf16[64,2048]{1,0:T(8,128)(2,1)S(1)}, bf16[64,2048]{1,0:T(8,128)(2,1)S(1)}, u32[]{:S(2)}, u32[]{:S(2)}) collective-permute-start(bf16[64,2048]{1,0:T(8,128)(2,1)S(1)} %bitcast_convert_fusion.own), channel_id=1, source_target_pairs={{0,8},{16,24},{32,40},{48,56},{64,72},{80,88},{96,104},{112,120},{... | collective-permute-start | bytes 786440 | tf_op jit(solution)/shard_map/ppermute | solution.py:392
  3.4 0.7 collective-permute-start.1
  4.1 0.0 collective-permute-done.2.core_copy
  4.1 1.1 %add_convert_fusion = bf16[64,2048]{1,0:T(8,128)(2,1)S(1)} fusion(bf16[64,2048]{1,0:T(8,128)(2,1)S(1)} %collective-permute-done.2.core_copy, f32[1,64,2048]{2,1,0:T(8,128)} %param.7), kind=kLoop, calls=%fused_computation | loop fusion | flops 393216 | bytes 1048576 | tf_op jit(solution)/shard_map/convert_element_type | solution.py:405
  5.2 6.3 %own_step.1 = (f32[64,1792]{1,0:T(8,128)S(1)}, bf16[1792,4096]{1,0:T(8,128)(2,1)S(1)}) custom-call(s32[1,8]{1,0:T(1,128)} %starts_in.5, bf16[64,2048]{1,0:T(8,128)(2,1)S(1)} %bitcast_convert_fusion.own, bf16[2048,4096]{1,0:T(8,128)(2,1)} %bitcast.19), custom_call_target="tpu_custom_call" | custom-call | flops 528482304 | bytes 14680064 | tf_op jit(solution)/shard_map/own_step/pallas_call | solution.py:88
  11.4 0.0 collective-permute-done.first
  11.5 0.0 collective-permute-done.1.second
  11.5 4.0 %collective-permute-start.3 = (bf16[64,2048]{1,0:T(8,128)(2,1)S(1)}, bf16[64,2048]{1,0:T(8,128)(2,1)S(1)}, u32[]{:S(2)}, u32[]{:S(2)}) collective-permute-start(bf16[64,2048]{1,0:T(8,128)(2,1)S(1)} %collective-permute-done.1.second), channel_id=1, source_target_pairs={{0,8},{16,24},{32,40},{48,56},{64,72},{80,88},{96,104},{112,120},{... | collective-permute-start | bytes 786440 | tf_op jit(solution)/shard_map/ppermute | solution.py:392
  15.5 0.7 collective-permute-start.4
  16.1 1.0 %collective-permute-start.5 = (bf16[64,2048]{1,0:T(8,128)(2,1)S(1)}, bf16[64,2048]{1,0:T(8,128)(2,1)S(1)}, u32[]{:S(2)}, u32[]{:S(2)}) collective-permute-start(bf16[64,2048]{1,0:T(8,128)(2,1)S(1)} %add_convert_fusion), channel_id=1, source_target_pairs={{0,4},{2,6},{4,0},{6,2},{1,5},{3,7},{5,1},{7,3},{8,12},{10,14},{12... | collective-permute-start | bytes 786440 | tf_op jit(solution)/shard_map/ppermute | solution.py:392
  17.1 5.8 %near_step.1 = (f32[64,2048]{1,0:T(8,128)S(1)}, bf16[256,4096]{1,0:T(8,128)(2,1)S(1)}) custom-call(s32[1,8]{1,0:T(1,128)} %starts_in.5, bf16[64,2048]{1,0:T(8,128)(2,1)S(1)} %bitcast_convert_fusion.own, bf16[64,2048]{1,0:T(8,128)(2,1)S(1)} %collective-permute-done.first, bf16[64,2048]{1,0:T(8,128)(2,1)S(1)} %collective-permute-done.1.second, ...), custom_call_target="tpu_custom_call" | custom-call | flops 1073741824 | bytes 3145728 | tf_op jit(solution)/shard_map/near_step/pallas_call | solution.py:173
  22.9 0.0 slice-start
  22.9 0.0 copy-start.3
  22.9 0.0 collective-permute-done.3.first
  22.9 0.0 collective-permute-done.4.second
  22.9 1.1 %collective-permute-done.5.pair_copy = bf16[64,2048]{1,0:T(8,128)(2,1)S(1)} collective-permute-done((bf16[64,2048]{1,0:T(8,128)(2,1)S(1)}, bf16[64,2048]{1,0:T(8,128)(2,1)S(1)}, u32[]{:S(2)}, u32[]{:S(2)}) %collective-permute-start.5) | collective-permute-done | bytes 262176 | tf_op jit(solution)/shard_map/ppermute | solution.py:392
  24.0 0.0 slice-start.1
  24.1 2.5 %far_step.1 = (f32[64,2048]{1,0:T(8,128)S(1)}, f32[64,128]{1,0:T(8,128)S(1)}) custom-call(s32[1,8]{1,0:T(1,128)} %starts_in.5, bf16[64,2048]{1,0:T(8,128)(2,1)S(1)} %collective-permute-done.3.first, bf16[64,2048]{1,0:T(8,128)(2,1)S(1)} %collective-permute-done.4.second, bf16[1792,4096]{1,0:T(8,128)(2,1)S(1)} %get-tuple-element.19.early, ...), custom_call_target="tpu_custom_call" | custom-call | flops 268435456 | bytes 2621440 | tf_op jit(solution)/shard_map/far_step/pallas_call | solution.py:276
  26.6 29.4 %all_to_all.10 = f32[64,1,128]{2,1,0:T(1,128)S(1)} all-to-all(f32[64,1,128]{2,1,0:T(1,128)S(1)} %bitcast.18), channel_id=1, replica_groups=mesh['genome'=32,'anc'=4,'trait'=2] {'genome','trait'}, dimensions={0} | all-to-all | bytes 65536 | tf_op jit(solution)/shard_map/all_to_all | solution.py:418
  56.0 4.5 %score_step.1 = (f32[64,2048]{1,0:T(8,128)}, bf16[32,32,128]{2,1,0:T(8,128)(2,1)S(1)}) custom-call(f32[64,128]{1,0:T(8,128)S(1)} %bitcast.17, f32[1,64]{1,0:T(1,128)S(1)} %copy-done.3, s32[1,2048]{1,0:T(1,128)S(1)} %copy-done.2, f32[64,2048]{1,0:T(8,128)S(1)} %get-tuple-element.25.proposal, bf16[2048,2048]{1,0:T(8,128)(2,1)S(1)} %bitcast.14), custom_call_target="tpu_custom_call" | custom-call | flops 536870912 | bytes 9437184 | tf_op jit(solution)/shard_map/score_step/pallas_call | solution.py:349
  60.5 15.5 %all_to_all.11.arrived = bf16[32,32,128]{2,1,0:T(8,128)(2,1)} all-to-all(bf16[32,32,128]{2,1,0:T(8,128)(2,1)S(1)} %get-tuple-element.27), channel_id=1, replica_groups=mesh['genome'=32,'anc'=4,'trait'=2] {'genome'}, dimensions={0} | all-to-all | bytes 524288 | tf_op jit(solution)/shard_map/all_to_all | solution.py:422
  75.9 1.7 %total_step.1 = f32[64,64]{1,0:T(8,128)} custom-call(bf16[32,32,128]{2,1,0:T(8,128)(2,1)} %all_to_all.11.arrived), custom_call_target="tpu_custom_call" | custom-call | tf_op jit(solution)/shard_map/total_step/pallas_call | solution.py:380
  (10 shorter events, 0.0 us)
Async XLA Ops:
  1.7 2.4 %collective-permute-start.2 = (bf16[64,2048]{1,0:T(8,128)(2,1)S(1)}, bf16[64,2048]{1,0:T(8,128)(2,1)S(1)}, u32[]{:S(2)}, u32[]{:S(2)}) collective-permute-start(bf16[64,2048]{1,0:T(8,128)(2,1)S(1)} %bitcast_convert_fusion.own), channel_id=1, source_target_pairs={{0,2},{4,6},{2,0},{6,4},{1,3},{5,7},{3,1},{7,5},{8,10},{12,14},{10... | collective-permute-start | bytes 786440 | tf_op jit(solution)/shard_map/ppermute | solution.py:392
  1.8 9.6 %collective-permute-start = (bf16[64,2048]{1,0:T(8,128)(2,1)S(1)}, bf16[64,2048]{1,0:T(8,128)(2,1)S(1)}, u32[]{:S(2)}, u32[]{:S(2)}) collective-permute-start(bf16[64,2048]{1,0:T(8,128)(2,1)S(1)} %bitcast_convert_fusion.own), channel_id=1, source_target_pairs={{0,8},{16,24},{32,40},{48,56},{64,72},{80,88},{96,104},{112,120},{... | collective-permute-start | bytes 786440 | tf_op jit(solution)/shard_map/ppermute | solution.py:392
  3.4 8.1 %collective-permute-start.1 = (bf16[64,2048]{1,0:T(8,128)(2,1)S(1)}, bf16[64,2048]{1,0:T(8,128)(2,1)S(1)}, u32[]{:S(2)}, u32[]{:S(2)}) collective-permute-start(bf16[64,2048]{1,0:T(8,128)(2,1)S(1)} %bitcast_convert_fusion.own), channel_id=1, source_target_pairs={{8,16},{24,32},{40,48},{56,64},{72,80},{88,96},{104,112},{120,128}... | collective-permute-start | bytes 786440 | tf_op jit(solution)/shard_map/ppermute | solution.py:392
  11.5 11.5 %collective-permute-start.3 = (bf16[64,2048]{1,0:T(8,128)(2,1)S(1)}, bf16[64,2048]{1,0:T(8,128)(2,1)S(1)}, u32[]{:S(2)}, u32[]{:S(2)}) collective-permute-start(bf16[64,2048]{1,0:T(8,128)(2,1)S(1)} %collective-permute-done.1.second), channel_id=1, source_target_pairs={{0,8},{16,24},{32,40},{48,56},{64,72},{80,88},{96,104},{112,120},{... | collective-permute-start | bytes 786440 | tf_op jit(solution)/shard_map/ppermute | solution.py:392
  15.5 7.5 %collective-permute-start.4 = (bf16[64,2048]{1,0:T(8,128)(2,1)S(1)}, bf16[64,2048]{1,0:T(8,128)(2,1)S(1)}, u32[]{:S(2)}, u32[]{:S(2)}) collective-permute-start(bf16[64,2048]{1,0:T(8,128)(2,1)S(1)} %collective-permute-done.first), channel_id=1, source_target_pairs={{8,16},{24,32},{40,48},{56,64},{72,80},{88,96},{104,112},{120,128}... | collective-permute-start | bytes 786440 | tf_op jit(solution)/shard_map/ppermute | solution.py:392
  16.1 7.9 %collective-permute-start.5 = (bf16[64,2048]{1,0:T(8,128)(2,1)S(1)}, bf16[64,2048]{1,0:T(8,128)(2,1)S(1)}, u32[]{:S(2)}, u32[]{:S(2)}) collective-permute-start(bf16[64,2048]{1,0:T(8,128)(2,1)S(1)} %add_convert_fusion), channel_id=1, source_target_pairs={{0,4},{2,6},{4,0},{6,2},{1,5},{3,7},{5,1},{7,3},{8,12},{10,14},{12... | collective-permute-start | bytes 786440 | tf_op jit(solution)/shard_map/ppermute | solution.py:392
  17.1 6.9 %copy-start = (f32[1,64,2048]{2,1,0:T(8,128)S(1)}, f32[1,64,2048]{2,1,0:T(8,128)}, u32[]{:S(2)}) copy-start(f32[1,64,2048]{2,1,0:T(8,128)} %param.7) | copy-start | bytes 1572868
  17.1 6.9 %copy-start.1 = (f32[1,64,2048]{2,1,0:T(8,128)S(1)}, f32[1,64,2048]{2,1,0:T(8,128)}, u32[]{:S(2)}) copy-start(f32[1,64,2048]{2,1,0:T(8,128)} %param.8) | copy-start | bytes 1572868
  17.1 6.9 %copy-start.2 = (s32[1,2048]{1,0:T(1,128)S(1)}, s32[1,2048]{1,0:T(1,128)}, u32[]{:S(2)}) copy-start(s32[1,2048]{1,0:T(1,128)} %ids.3) | copy-start | bytes 24580
  22.9 33.1 %slice-start = ((s8[8388608]{0:T(1024)(128)(4,1)}), s8[4194304]{0:T(1024)(128)(4,1)S(1)}, s32[]{:S(2)}) async-start(s8[8388608]{0:T(1024)(128)(4,1)} %bitcast.12), calls=%async_computation.2 | async-start | bytes 8388608
  22.9 33.1 %copy-start.3 = (f32[1,64]{1,0:T(1,128)S(1)}, f32[1,64]{1,0:T(1,128)}, u32[]{:S(2)}) copy-start(f32[1,64]{1,0:T(1,128)} %weights.1) | copy-start | bytes 772
  24.0 31.9 %slice-start.1 = ((s8[8388608]{0:T(1024)(128)(4,1)}), s8[4194304]{0:T(1024)(128)(4,1)S(1)}, s32[]{:S(2)}) async-start(s8[8388608]{0:T(1024)(128)(4,1)} %bitcast.12), calls=%async_computation.3 | async-start | bytes 8388608

commit v6 on v5

--- a/solution.py
+++ b/solution.py
@@ -12,6 +12,7 @@
 LANES = 128
 GROUPS = 64
 EARLY = 7
+FIRST_HALF = 4
 
 step_size = 0.5
 merging = 0.5
@@ -107,17 +108,33 @@
     )(pltpu.with_memory_space_constraint(starts, pltpu.HBM), own, pltpu.with_memory_space_constraint(band, pltpu.HBM))
 
 
-def near_kernel(
-    starts_in, own, first, second, early, before, band, product, late, extended, starts, sems, start_sem
+def half_kernel(from_unit, to_unit, starts_in, first, second, early, before, product, extended, starts, start_sem):
+    near_body(
+        from_unit, to_unit, starts_in, None, first, second, early, before, None, product, None, extended, starts,
+        None, start_sem,
+    )
+
+
+def rest_kernel(
+    from_unit, starts_in, own, first, second, early, before, band, product, late, extended, starts, sems, start_sem
+):
+    near_body(
+        from_unit, first.shape[1] // TILE, starts_in, own, first, second, early, before, band, product, late,
+        extended, starts, sems, start_sem,
+    )
+
+
+def near_body(
+    from_unit, to_unit, starts_in, own, first, second, early, before, band, product, late, extended, starts, sems,
+    start_sem,
 ):
     rows, snps = first.shape
-    width = band.shape[1]
-    units = snps // TILE
-    early_units = early.shape[0] // TILE
-    count = units + 1
+    width = early.shape[1]
+    early_units = min(early.shape[0] // TILE, to_unit)
+    count = snps // TILE + 1
     start_copy = pltpu.make_async_copy(starts_in, starts, start_sem)
     start_copy.start()
-    for unit in range(early_units, units):
+    for unit in range(early_units, to_unit):
         unit_copy(band, late, sems, unit, early_units).start()
     place = place_of()
     first_at = jnp.where(lax.rem(place, 2) == 0, 3 * snps, snps)
@@ -145,10 +162,12 @@
             base = pl.multiple_of((begin // LANES) * LANES, LANES)
             window = window_tiles(extended, base, begin - base, TILE // LANES)
             total += lax.dot_general(window, early[cut, pl.ds(column, TILE)], NT, preferred_element_type=jnp.float32)
-        product[:, cut] = total
+        product[:, pl.ds(pl.multiple_of((unit - from_unit) * TILE, TILE), TILE)] = total
         return carry
 
-    lax.fori_loop(0, early_units, early_unit, 0)
+    lax.fori_loop(from_unit, early_units, early_unit, 0)
+    if own is None:
+        return
     extended[:, 2 * snps : 3 * snps] = own[...].astype(jnp.float32)
 
     def late_unit(unit, carry):
@@ -157,25 +176,47 @@
         window = window_tiles(extended, base, start - base, width // LANES)
         unit_copy(band, late, sems, unit, early_units).wait()
         here = pl.ds(pl.multiple_of((unit - early_units) * TILE, TILE), TILE)
-        cut = pl.ds(pl.multiple_of(unit * TILE, TILE), TILE)
+        cut = pl.ds(pl.multiple_of((unit - from_unit) * TILE, TILE), TILE)
         product[:, cut] = lax.dot_general(window, late[here, :], NT, preferred_element_type=jnp.float32)
         return carry
 
-    lax.fori_loop(early_units, units, late_unit, 0)
-
-
-def near_step(starts, own, first, second, early, before, band):
+    lax.fori_loop(early_units, to_unit, late_unit, 0)
+
+
+def half_step(starts, first, second, early, before, to_unit):
+    rows, snps = first.shape
+    hbm = pl.BlockSpec(memory_space=pltpu.HBM)
+    vmem = pl.BlockSpec(memory_space=pltpu.VMEM)
+    return pl.pallas_call(
+        functools.partial(half_kernel, 0, to_unit),
+        in_specs=[hbm] + [vmem] * 4,
+        out_specs=vmem,
+        out_shape=jax.ShapeDtypeStruct((rows, to_unit * TILE), jnp.float32),
+        scratch_shapes=[
+            pltpu.VMEM((rows, 5 * snps + LANES), jnp.float32),
+            pltpu.SMEM((1, snps // TILE), jnp.int32),
+            pltpu.SemaphoreType.DMA,
+        ],
+        compiler_params=pltpu.CompilerParams(vmem_limit_bytes=10 << 20),
+        cost_estimate=pl.CostEstimate(
+            flops=2 * rows * to_unit * TILE * (snps + TILE), bytes_accessed=8 * rows * snps, transcendentals=0
+        ),
+        name="half_step",
+    )(pltpu.with_memory_space_constraint(starts, pltpu.HBM), first, second, early, before)
+
+
+def near_step(starts, own, first, second, early, before, band, from_unit):
     rows, snps = first.shape
     width = band.shape[1]
     late_rows = snps - early.shape[0]
     hbm = pl.BlockSpec(memory_space=pltpu.HBM)
     vmem = pl.BlockSpec(memory_space=pltpu.VMEM)
     return pl.pallas_call(
-        near_kernel,
+        functools.partial(rest_kernel, from_unit),
         in_specs=[hbm] + [vmem] * 5 + [hbm],
         out_specs=[vmem, vmem],
         out_shape=[
-            jax.ShapeDtypeStruct((rows, snps), jnp.float32),
+            jax.ShapeDtypeStruct((rows, snps - from_unit * TILE), jnp.float32),
             jax.ShapeDtypeStruct((late_rows, width), band.dtype),
         ],
         scratch_shapes=[
@@ -196,7 +237,7 @@
 
 
 def far_kernel(
-    ancestries, starts_in, first, second, early, late, product, coef, targets, core_copy, pair_copy, ids,
+    ancestries, starts_in, first, second, early, late, product, rest, coef, targets, core_copy, pair_copy, ids,
     proposal, sums, far, square_acc, count_acc, bands_ref, starts, start_sem,
 ):
     rows, snps = coef.shape
@@ -216,7 +257,7 @@
     start_copy.wait()
     group = lax.broadcasted_iota(jnp.int32, (GROUPS, LANES), 0)
 
-    def per_unit(held, first_unit, unit, carry):
+    def per_unit(held, first_unit, before, before_unit, unit, carry):
         cut = pl.ds(pl.multiple_of(unit * TILE, TILE), TILE)
         here = pl.ds(pl.multiple_of((unit - first_unit) * TILE, TILE), TILE)
         start = starts[0, unit] + (2 - place) * snps
@@ -226,7 +267,7 @@
         above = high_count > 0
         needed = low_count + high_count
         choice = sum((needed > width).astype(jnp.int32) for width in widths[:-1])
-        bands_ref[...] = product[:, cut]
+        bands_ref[...] = before[:, pl.ds(pl.multiple_of((unit - before_unit) * TILE, TILE), TILE)]
         for option, width in enumerate(widths):
             if width == 0:
                 continue
@@ -260,8 +301,10 @@
         return carry
 
     early_units = early.shape[0] // TILE
-    lax.fori_loop(0, early_units, functools.partial(per_unit, early, 0), 0)
-    lax.fori_loop(early_units, units, functools.partial(per_unit, late, early_units), 0)
+    half_units = product.shape[1] // TILE
+    lax.fori_loop(0, half_units, functools.partial(per_unit, early, 0, product, 0), 0)
+    lax.fori_loop(half_units, early_units, functools.partial(per_unit, early, 0, rest, half_units), 0)
+    lax.fori_loop(early_units, units, functools.partial(per_unit, late, early_units, rest, half_units), 0)
     lane = lax.broadcasted_iota(jnp.int32, (GROUPS, LANES), 1)
     square_col = jnp.sum(square_acc[...], axis=1, keepdims=True)
     count_col = jnp.sum(count_acc[...], axis=1, keepdims=True)
@@ -269,13 +312,13 @@
     sums[...] = jnp.broadcast_to(jnp.sum(both, axis=0, keepdims=True), sums.shape)
 
 
-def far_step(starts, first, second, early, late, product, coef, targets, core_copy, pair_copy, ids, peers, ancestries):
+def far_step(starts, first, second, early, late, product, rest, coef, targets, core_copy, pair_copy, ids, peers, ancestries):
     rows, snps = coef.shape
     hbm = pl.BlockSpec(memory_space=pltpu.HBM)
     vmem = pl.BlockSpec(memory_space=pltpu.VMEM)
     return pl.pallas_call(
         functools.partial(far_kernel, ancestries),
-        in_specs=[hbm] + [vmem] * 10,
+        in_specs=[hbm] + [vmem] * 11,
         out_specs=[vmem, vmem],
         out_shape=[
             jax.ShapeDtypeStruct((rows, snps), jnp.float32),
@@ -295,7 +338,7 @@
         ),
         name="far_step",
     )(
-        pltpu.with_memory_space_constraint(starts, pltpu.HBM), first, second, early, late, product, coef, targets, core_copy, pair_copy, ids,
+        pltpu.with_memory_space_constraint(starts, pltpu.HBM), first, second, early, late, product, rest, coef, targets, core_copy, pair_copy, ids,
     )
 
 
@@ -408,11 +451,13 @@
     own_product, early = own_step(band_start, own_copy, band, EARLY)
     near_even, near_odd, own_product = lax.optimization_barrier((near_even, near_odd, own_product))
     far_even = swapped(near_odd, "genome", 1, lambda i: i % 2 == 0)
+    product = half_step(band_start, near_even, near_odd, early, own_product, FIRST_HALF)
+    near_even, near_odd, product = lax.optimization_barrier((near_even, near_odd, product))
     far_odd = swapped(near_even, "genome", 1, lambda i: i % 2 == 1)
-    product, late = near_step(band_start, low_copy, near_even, near_odd, early, own_product, band)
+    rest, late = near_step(band_start, low_copy, near_even, near_odd, early, own_product, band, FIRST_HALF)
     peers = genome_count * lax.axis_size("trait")
     proposal, sums = far_step(
-        band_start, far_even, far_odd, early, late, product, current, targets, core_copy, pair_copy,
+        band_start, far_even, far_odd, early, late, product, rest, current, targets, core_copy, pair_copy,
         group_ids, peers, anc_count,
     )
     arrived = lax.all_to_all(

time: 77.9 us -> 81.2 us (1.042)
  waiting for transfers between devices: 1.11 us -> 3.5 us
    ppermute x6, waiting for transfers between devices: 1.11 us -> 3.5 us  [swapped(): return lax.ppermute(block, axis, pairs + [(j, i) for i, j in pairs])]
    pallas_call x1 -> x2, Pallas kernels: 5.77 us -> 6.31 us  [the longest x1 3.38 us: near_step(): pl.pallas_call(functools.partial(rest_kernel, from_unit), in_specs=[hbm]...]
where the time goes in v6:
time: 81.2 us; the launch traced here: 80.3 us
  blocking collectives  45.1 us (56%)
  Pallas kernels  20.6 us (25%)
  starting transfers between devices  8.11 us (10%)
  waiting for transfers between devices  3.5 us (4%)
  other arithmetic  2.16 us (3%)
    all_to_all x1, blocking collectives, per_device(): lax.all_to_all(sums.reshape(peers, 1, LANES), ('genome', 'trait'), split_...  29.6 us
    all_to_all x1, blocking collectives, per_device(): lax.all_to_all(partial, 'genome', split_axis=0, concat_axis=0, tiled=True)  15.4 us
    ppermute x6, starting transfers between devices, swapped(): return lax.ppermute(block, axis, pairs + [(j, i) for i, j in pairs])  8.11 us
    pallas_call x1, Pallas kernels, own_step(): pl.pallas_call(own_kernel, in_specs=[hbm, vmem, hbm], out_specs=[vmem, vm...  6.27 us
    pallas_call x1, Pallas kernels, score_step(): pl.pallas_call(functools.partial(score_kernel, 1.0 / math.sqrt(snps * gen...  4.5 us
    ppermute x6, waiting for transfers between devices, swapped(): return lax.ppermute(block, axis, pairs + [(j, i) for i, j in pairs])  3.5 us
    pallas_call x1, Pallas kernels, near_step(): pl.pallas_call(functools.partial(rest_kernel, from_unit), in_specs=[hbm]...  3.38 us
    pallas_call x1, Pallas kernels, half_step(): pl.pallas_call(functools.partial(half_kernel, 0, to_unit), in_specs=[hbm]...  2.93 us
  transfers between devices with their start and end apart: 6, of which 1 were waited for; matrix products, arithmetic and copies ran while one was open for 1% of the time, Pallas kernels for 16%

profile of v6, /device:TPU:8, one launch (start us, length us, event | category | flops | bytes accessed | tf_op | source)
XLA Modules:
  0.0 80.3 jit_solution(8525679240722170547)
XLA Ops:
  0.6 1.1 %bitcast_convert_fusion.own = bf16[64,2048]{1,0:T(8,128)(2,1)S(1)} fusion(f32[1,64,2048]{2,1,0:T(8,128)} %param.7), kind=kLoop, calls=%fused_computation.1 | loop fusion | flops 131072 | bytes 786432 | tf_op jit(solution)/shard_map/convert_element_type | solution.py:444
  1.7 0.1 collective-permute-start.2
  1.8 1.6 %collective-permute-start = (bf16[64,2048]{1,0:T(8,128)(2,1)S(1)}, bf16[64,2048]{1,0:T(8,128)(2,1)S(1)}, u32[]{:S(2)}, u32[]{:S(2)}) collective-permute-start(bf16[64,2048]{1,0:T(8,128)(2,1)S(1)} %bitcast_convert_fusion.own), channel_id=1, source_target_pairs={{0,8},{16,24},{32,40},{48,56},{64,72},{80,88},{96,104},{112,120},{... | collective-permute-start | bytes 786440 | tf_op jit(solution)/shard_map/ppermute | solution.py:435
  3.4 0.7 collective-permute-start.1
  4.1 0.0 collective-permute-done.2.core_copy
  4.1 1.1 %add_convert_fusion = bf16[64,2048]{1,0:T(8,128)(2,1)S(1)} fusion(bf16[64,2048]{1,0:T(8,128)(2,1)S(1)} %collective-permute-done.2.core_copy, f32[1,64,2048]{2,1,0:T(8,128)} %param.7), kind=kLoop, calls=%fused_computation | loop fusion | flops 393216 | bytes 1048576 | tf_op jit(solution)/shard_map/convert_element_type | solution.py:448
  5.2 6.3 %own_step.1 = (f32[64,1792]{1,0:T(8,128)S(1)}, bf16[1792,4096]{1,0:T(8,128)(2,1)S(1)}) custom-call(s32[1,8]{1,0:T(1,128)} %starts_in.7, bf16[64,2048]{1,0:T(8,128)(2,1)S(1)} %bitcast_convert_fusion.own, bf16[2048,4096]{1,0:T(8,128)(2,1)} %bitcast.19), custom_call_target="tpu_custom_call" | custom-call | flops 528482304 | bytes 14680064 | tf_op jit(solution)/shard_map/own_step/pallas_call | solution.py:89
  11.5 0.0 collective-permute-done.1.second
  11.5 4.0 %collective-permute-start.3 = (bf16[64,2048]{1,0:T(8,128)(2,1)S(1)}, bf16[64,2048]{1,0:T(8,128)(2,1)S(1)}, u32[]{:S(2)}, u32[]{:S(2)}) collective-permute-start(bf16[64,2048]{1,0:T(8,128)(2,1)S(1)} %collective-permute-done.1.second), channel_id=1, source_target_pairs={{0,8},{16,24},{32,40},{48,56},{64,72},{80,88},{96,104},{112,120},{... | collective-permute-start | bytes 786440 | tf_op jit(solution)/shard_map/ppermute | solution.py:435
  15.5 2.9 %half_step.1.product = f32[64,1024]{1,0:T(8,128)S(1)} custom-call(s32[1,8]{1,0:T(1,128)} %starts_in.7, bf16[64,2048]{1,0:T(8,128)(2,1)S(1)} %collective-permute-done.first, bf16[64,2048]{1,0:T(8,128)(2,1)S(1)} %collective-permute-done.1.second, bf16[1792,4096]{1,0:T(8,128)(2,1)S(1)} %get-tuple-element.22.early, f32[64,1792]{1,0:T(8,128)S(1)} %get-tuple-element.23.before), custom_call_target="tpu_custom_call" | custom-call | flops 301989888 | bytes 1048576 | tf_op jit(solution)/shard_map/half_step/pallas_call | solution.py:190
  18.4 0.0 copy-start
  18.4 0.0 copy-start.1
  18.4 0.0 copy-start.2
  18.4 0.8 %collective-permute-start.4 = (bf16[64,2048]{1,0:T(8,128)(2,1)S(1)}, bf16[64,2048]{1,0:T(8,128)(2,1)S(1)}, u32[]{:S(2)}, u32[]{:S(2)}) collective-permute-start(bf16[64,2048]{1,0:T(8,128)(2,1)S(1)} %collective-permute-done.first), channel_id=1, source_target_pairs={{8,16},{24,32},{40,48},{56,64},{72,80},{88,96},{104,112},{120,128}... | collective-permute-start | bytes 786440 | tf_op jit(solution)/shard_map/ppermute | solution.py:435
  19.3 1.0 %collective-permute-start.5 = (bf16[64,2048]{1,0:T(8,128)(2,1)S(1)}, bf16[64,2048]{1,0:T(8,128)(2,1)S(1)}, u32[]{:S(2)}, u32[]{:S(2)}) collective-permute-start(bf16[64,2048]{1,0:T(8,128)(2,1)S(1)} %add_convert_fusion), channel_id=1, source_target_pairs={{0,4},{2,6},{4,0},{6,2},{1,5},{3,7},{5,1},{7,3},{8,12},{10,14},{12... | collective-permute-start | bytes 786440 | tf_op jit(solution)/shard_map/ppermute | solution.py:435
  20.2 3.4 %near_step.1 = (f32[64,1024]{1,0:T(8,128)S(1)}, bf16[256,4096]{1,0:T(8,128)(2,1)S(1)}) custom-call(s32[1,8]{1,0:T(1,128)} %starts_in.7, bf16[64,2048]{1,0:T(8,128)(2,1)S(1)} %bitcast_convert_fusion.own, bf16[64,2048]{1,0:T(8,128)(2,1)S(1)} %collective-permute-done.first, bf16[64,2048]{1,0:T(8,128)(2,1)S(1)} %collective-permute-done.1.second, ...), custom_call_target="tpu_custom_call" | custom-call | flops 1073741824 | bytes 3145728 | tf_op jit(solution)/shard_map/near_step/pallas_call | solution.py:214
  23.6 0.0 slice-start
  23.6 0.0 copy-start.3
  23.7 3.5 %collective-permute-done.5.pair_copy = bf16[64,2048]{1,0:T(8,128)(2,1)S(1)} collective-permute-done((bf16[64,2048]{1,0:T(8,128)(2,1)S(1)}, bf16[64,2048]{1,0:T(8,128)(2,1)S(1)}, u32[]{:S(2)}, u32[]{:S(2)}) %collective-permute-start.5) | collective-permute-done | bytes 262176 | tf_op jit(solution)/shard_map/ppermute | solution.py:435
  27.2 1.8 %far_step.1 = (f32[64,2048]{1,0:T(8,128)S(1)}, f32[64,128]{1,0:T(8,128)S(1)}) custom-call(s32[1,8]{1,0:T(1,128)} %starts_in.7, bf16[64,2048]{1,0:T(8,128)(2,1)S(1)} %collective-permute-done.3.first, bf16[64,2048]{1,0:T(8,128)(2,1)S(1)} %collective-permute-done.4.second, bf16[1792,4096]{1,0:T(8,128)(2,1)S(1)} %get-tuple-element.22.early, ...), custom_call_target="tpu_custom_call" | custom-call | flops 268435456 | bytes 2621440 | tf_op jit(solution)/shard_map/far_step/pallas_call | solution.py:319
  29.0 29.6 %all_to_all.10 = f32[64,1,128]{2,1,0:T(1,128)S(1)} all-to-all(f32[64,1,128]{2,1,0:T(1,128)S(1)} %bitcast.18), channel_id=1, replica_groups=mesh['genome'=32,'anc'=4,'trait'=2] {'genome','trait'}, dimensions={0} | all-to-all | bytes 65536 | tf_op jit(solution)/shard_map/all_to_all | solution.py:463
  58.6 4.5 %score_step.1 = (f32[64,2048]{1,0:T(8,128)}, bf16[32,32,128]{2,1,0:T(8,128)(2,1)S(1)}) custom-call(f32[64,128]{1,0:T(8,128)S(1)} %bitcast.17, f32[1,64]{1,0:T(1,128)S(1)} %copy-done.3, s32[1,2048]{1,0:T(1,128)S(1)} %copy-done.2, f32[64,2048]{1,0:T(8,128)S(1)} %get-tuple-element.31.proposal, bf16[2048,2048]{1,0:T(8,128)(2,1)S(1)} %bitcast.14), custom_call_target="tpu_custom_call" | custom-call | flops 536870912 | bytes 9437184 | tf_op jit(solution)/shard_map/score_step/pallas_call | solution.py:392
  63.2 15.4 %all_to_all.11.arrived = bf16[32,32,128]{2,1,0:T(8,128)(2,1)} all-to-all(bf16[32,32,128]{2,1,0:T(8,128)(2,1)S(1)} %get-tuple-element.33), channel_id=1, replica_groups=mesh['genome'=32,'anc'=4,'trait'=2] {'genome'}, dimensions={0} | all-to-all | bytes 524288 | tf_op jit(solution)/shard_map/all_to_all | solution.py:467
  78.6 1.7 %total_step.1 = f32[64,64]{1,0:T(8,128)} custom-call(bf16[32,32,128]{2,1,0:T(8,128)(2,1)} %all_to_all.11.arrived), custom_call_target="tpu_custom_call" | custom-call | tf_op jit(solution)/shard_map/total_step/pallas_call | solution.py:423
  (11 shorter events, 0.0 us)
Async XLA Ops:
  1.7 2.4 %collective-permute-start.2 = (bf16[64,2048]{1,0:T(8,128)(2,1)S(1)}, bf16[64,2048]{1,0:T(8,128)(2,1)S(1)}, u32[]{:S(2)}, u32[]{:S(2)}) collective-permute-start(bf16[64,2048]{1,0:T(8,128)(2,1)S(1)} %bitcast_convert_fusion.own), channel_id=1, source_target_pairs={{0,2},{4,6},{2,0},{6,4},{1,3},{5,7},{3,1},{7,5},{8,10},{12,14},{10... | collective-permute-start | bytes 786440 | tf_op jit(solution)/shard_map/ppermute | solution.py:435
  1.8 9.6 %collective-permute-start = (bf16[64,2048]{1,0:T(8,128)(2,1)S(1)}, bf16[64,2048]{1,0:T(8,128)(2,1)S(1)}, u32[]{:S(2)}, u32[]{:S(2)}) collective-permute-start(bf16[64,2048]{1,0:T(8,128)(2,1)S(1)} %bitcast_convert_fusion.own), channel_id=1, source_target_pairs={{0,8},{16,24},{32,40},{48,56},{64,72},{80,88},{96,104},{112,120},{... | collective-permute-start | bytes 786440 | tf_op jit(solution)/shard_map/ppermute | solution.py:435
  3.4 8.1 %collective-permute-start.1 = (bf16[64,2048]{1,0:T(8,128)(2,1)S(1)}, bf16[64,2048]{1,0:T(8,128)(2,1)S(1)}, u32[]{:S(2)}, u32[]{:S(2)}) collective-permute-start(bf16[64,2048]{1,0:T(8,128)(2,1)S(1)} %bitcast_convert_fusion.own), channel_id=1, source_target_pairs={{8,16},{24,32},{40,48},{56,64},{72,80},{88,96},{104,112},{120,128}... | collective-permute-start | bytes 786440 | tf_op jit(solution)/shard_map/ppermute | solution.py:435
  11.5 12.2 %collective-permute-start.3 = (bf16[64,2048]{1,0:T(8,128)(2,1)S(1)}, bf16[64,2048]{1,0:T(8,128)(2,1)S(1)}, u32[]{:S(2)}, u32[]{:S(2)}) collective-permute-start(bf16[64,2048]{1,0:T(8,128)(2,1)S(1)} %collective-permute-done.1.second), channel_id=1, source_target_pairs={{0,8},{16,24},{32,40},{48,56},{64,72},{80,88},{96,104},{112,120},{... | collective-permute-start | bytes 786440 | tf_op jit(solution)/shard_map/ppermute | solution.py:435
  18.4 8.7 %copy-start = (f32[1,64,2048]{2,1,0:T(8,128)S(1)}, f32[1,64,2048]{2,1,0:T(8,128)}, u32[]{:S(2)}) copy-start(f32[1,64,2048]{2,1,0:T(8,128)} %param.7) | copy-start | bytes 1572868
  18.4 8.7 %copy-start.1 = (f32[1,64,2048]{2,1,0:T(8,128)S(1)}, f32[1,64,2048]{2,1,0:T(8,128)}, u32[]{:S(2)}) copy-start(f32[1,64,2048]{2,1,0:T(8,128)} %param.8) | copy-start | bytes 1572868
  18.4 8.7 %copy-start.2 = (s32[1,2048]{1,0:T(1,128)S(1)}, s32[1,2048]{1,0:T(1,128)}, u32[]{:S(2)}) copy-start(s32[1,2048]{1,0:T(1,128)} %ids.3) | copy-start | bytes 24580
  18.4 5.2 %collective-permute-start.4 = (bf16[64,2048]{1,0:T(8,128)(2,1)S(1)}, bf16[64,2048]{1,0:T(8,128)(2,1)S(1)}, u32[]{:S(2)}, u32[]{:S(2)}) collective-permute-start(bf16[64,2048]{1,0:T(8,128)(2,1)S(1)} %collective-permute-done.first), channel_id=1, source_target_pairs={{8,16},{24,32},{40,48},{56,64},{72,80},{88,96},{104,112},{120,128}... | collective-permute-start | bytes 786440 | tf_op jit(solution)/shard_map/ppermute | solution.py:435
  19.3 7.9 %collective-permute-start.5 = (bf16[64,2048]{1,0:T(8,128)(2,1)S(1)}, bf16[64,2048]{1,0:T(8,128)(2,1)S(1)}, u32[]{:S(2)}, u32[]{:S(2)}) collective-permute-start(bf16[64,2048]{1,0:T(8,128)(2,1)S(1)} %add_convert_fusion), channel_id=1, source_target_pairs={{0,4},{2,6},{4,0},{6,2},{1,5},{3,7},{5,1},{7,3},{8,12},{10,14},{12... | collective-permute-start | bytes 786440 | tf_op jit(solution)/shard_map/ppermute | solution.py:435
  23.6 35.0 %slice-start = ((s8[8388608]{0:T(1024)(128)(4,1)}), s8[4194304]{0:T(1024)(128)(4,1)S(1)}, s32[]{:S(2)}) async-start(s8[8388608]{0:T(1024)(128)(4,1)} %bitcast.12), calls=%async_computation.2 | async-start | bytes 8388608
  23.6 35.0 %copy-start.3 = (f32[1,64]{1,0:T(1,128)S(1)}, f32[1,64]{1,0:T(1,128)}, u32[]{:S(2)}) copy-start(f32[1,64]{1,0:T(1,128)} %weights.1) | copy-start | bytes 772
  27.2 31.5 %slice-start.1 = ((s8[8388608]{0:T(1024)(128)(4,1)}), s8[4194304]{0:T(1024)(128)(4,1)S(1)}, s32[]{:S(2)}) async-start(s8[8388608]{0:T(1024)(128)(4,1)} %bitcast.12), calls=%async_computation.3 | async-start | bytes 8388608
